TPU v7x, 512 devices: a whole 4x8x8 slice. The times are simulated.
512 devices in a mesh: wide: 64 (over z, y_hi, core), narrow: 8 (over x, y_lo).
Axes of the slice: x: 4, y: 8 (y_hi: 4, y_lo: 2; y = y_hi * 2 + y_lo), z: 8, core: 2. Of those that a mesh axis runs over, the one named last changes fastest.
Arguments:
- positions: float32 [3, 131072], P(None, ('wide', 'narrow')), may hold values from 0 to 1
- volumes: float32 [131072], P(('wide', 'narrow')), may hold values from 0.5 to 2
- phase_field: float32 [131072], P(('wide', 'narrow')), may hold values from -1 to 1.4
- stencil_weights: float32 [64, 131072], P(None, ('wide', 'narrow')), may hold values from 0.005 to 0.05
- stencil_slots: int32 [64, 131072], P(None, ('wide', 'narrow')), may hold values from 0 to 767, as said below
- send_lists: int32 [2, 131072], P(None, ('wide', 'narrow')), may hold values from 0 to 255, as said below
Outputs:
- phase_next: float32 [131072], P(('wide', 'narrow'))
- potential_next: float32 [131072], P(('wide', 'narrow'))
Inputs may be any that keep to these rules, and one draw needn't show every extreme that they name: `stencil_slots`: entry k of point i names a neighbour in ext of i's block: values below 256 are rows of the same block other than i; 256 + s is slot s of the list that the block one lower along wide (cyclically) sends up, 512 + s slot s of the list that the block one higher sends down; s is always below that list's count c, and every slot below c is named by some point of the receiving block. `send_lists`: each block's list in each row has a count c of 1 to 256: its first c slots hold distinct rows of 0 to 255 and the rest hold 0; in each row some block's list is full.
All inputs are finite; a program needn't handle non-finite values.
Results may differ from a plain program's by a relative error of at most 0.00002.
Values sent between devices are 32-bit elements; how exact they have to be, the bound alone decides.
A program may use at most 64 MiB of HBM per device.

v0:
```python
import jax
import jax.numpy as jnp
from jax import lax
from jax.sharding import PartitionSpec as P

kernel_strength = 0.1
gradient_energy = 0.5
time_step = 0.2


def padded(cells, sides, width):
    for axis, dim in sides:
        count = lax.axis_size(axis)
        head = lax.slice_in_dim(cells, 0, width, axis=dim)
        tail = lax.slice_in_dim(cells, cells.shape[dim] - width, cells.shape[dim], axis=dim)
        cells = jnp.concatenate(
            [
                lax.ppermute(tail, axis, [(i, (i + 1) % count) for i in range(count)]),
                cells,
                lax.ppermute(head, axis, [((i + 1) % count, i) for i in range(count)]),
            ],
            axis=dim,
        )
    return cells


def add_sources(totals, targets, sources, vols, values, kernel_decay):
    count_src = values.shape[0]
    block_len = 512

    def add_block(turn, partial_sums):
        offset = turn * block_len
        src_block = lax.dynamic_slice_in_dim(sources, offset, block_len, 1)
        vol_block = lax.dynamic_slice_in_dim(vols, offset, block_len, 0)
        val_block = lax.dynamic_slice_in_dim(values, offset, block_len, 0)
        distance = (targets[0][:, None] - src_block[0][None, :]) ** 2
        distance = distance + (targets[1][:, None] - src_block[1][None, :]) ** 2
        distance = distance + (targets[2][:, None] - src_block[2][None, :]) ** 2
        gauss_vol = jnp.exp(-kernel_decay * distance) * vol_block[None, :]
        return (
            partial_sums[0] + jnp.sum(gauss_vol, axis=1),
            partial_sums[1] + jnp.sum(gauss_vol * val_block[None, :], axis=1),
        )

    return lax.fori_loop(0, count_src // block_len, add_block, totals)


def shards(positions, volumes, phase_field, stencil_weights, stencil_slots, send_lists):
    own_rows = phase_field.shape[0]
    send_len = send_lists.shape[1]
    patch_len = own_rows * lax.axis_size("narrow")
    kernel_decay = 0.5 * float(patch_len) ** (2.0 / 3.0)
    packet_rows = jnp.concatenate([send_lists[1], send_lists[0]])

    def extend(field_now):
        rim_values = padded(field_now[packet_rows], (("wide", 0),), send_len)
        return jnp.concatenate([field_now, rim_values[:send_len], rim_values[-send_len:]])

    zero_sums = (jnp.zeros((own_rows,), jnp.float32), jnp.zeros((own_rows,), jnp.float32))

    def kernel_totals(field_now):
        stacked = jnp.concatenate([positions, volumes[None, :], field_now[None, :]], axis=0)
        part_rows = lax.all_gather(stacked, "narrow", axis=1, tiled=True)
        return add_sources(
            zero_sums, positions, part_rows[:3], part_rows[3], part_rows[4], kernel_decay
        )

    def laplace(field_now):
        extended = extend(field_now)
        neighbour_vals = extended[stencil_slots]
        return jnp.sum(stencil_weights * (neighbour_vals - field_now[None, :]), axis=0)

    def potential(field_now):
        sum_mass, sum_field = kernel_totals(field_now)
        kernel_term = kernel_strength * sum_mass * field_now - kernel_strength * sum_field
        return field_now**3 - field_now + kernel_term - gradient_energy * laplace(field_now)

    potential_now = potential(phase_field)
    phase_next = phase_field + time_step * laplace(potential_now)
    return (phase_next, potential(phase_next))


def solution(mesh):
    placed = (
        P(None, ("wide", "narrow")),
        P(("wide", "narrow")),
        P(("wide", "narrow")),
        P(None, ("wide", "narrow")),
        P(None, ("wide", "narrow")),
        P(None, ("wide", "narrow")),
    )
    return jax.shard_map(
        shards,
        mesh=mesh,
        in_specs=placed,
        out_specs=(P(("wide", "narrow")), P(("wide", "narrow"))),
        check_vma=False,
    )
```

profile of v0, /device:TPU:14, one launch (start us, length us, event | category | flops | bytes accessed | tf_op | source)
XLA Modules:
  0.0 310.7 jit_solution(3009720424811803415)
XLA Ops:
  0.6 0.8 slice_bitcast_fusion.1
  1.4 0.7 copy-done
  2.1 3.5 %gather_fusion = f32[512]{0:T(512)S(1)} fusion(f32[256]{0:T(256)S(1)} %copy-done, s32[1024]{0:T(1024)S(1)} %pad_clamp_fusion), kind=kCustom, calls=%fused_computation | custom fusion | bytes 6144 | tf_op jit(solution)/shard_map/gather | solution.py:56
  5.6 0.0 copy-start.3
  5.6 1.9 collective-permute-start
  7.5 13.2 %collective-permute-start.1 = (f32[256]{0:T(256)S(1)}, f32[256]{0:T(256)S(1)}, u32[]{:S(2)}, u32[]{:S(2)}) collective-permute-start(f32[256]{0:T(256)S(1)} %get-tuple-element.361), channel_id=1, source_target_pairs={{8,0},{16,8},{24,16},{32,24},{40,32},{48,40},{56,48},{64,56},{72,6... | collective-permute-start | bytes 3080 | tf_op jit(solution)/shard_map/ppermute | solution.py:20
  20.7 0.0 copy-start.6
  20.7 0.7 copy-done.6
  21.4 28.3 %all_gather.6 = f32[5,2048]{1,0:T(8,128)S(1)} all-gather(f32[5,256]{1,0:T(8,128)S(1)} %pad_maximum_fusion), channel_id=1, replica_groups=mesh['wide'=64,'narrow'=8] {'narrow'}, dimensions={1}, use_global_device_ids=true | all-gather | bytes 46080 | tf_op jit(solution)/shard_map/all_gather | solution.py:63
  49.7 0.6 copy-done.4
  50.3 0.2 copy-done.5
  50.5 0.0 slice-start
  50.6 0.7 slice-done
  51.3 2.8 while.32
  51.3 0.1 constant_dynamic-slice_fusion.4
  51.4 0.1 dynamic_slice.52
  51.4 0.1 dynamic_slice.53
  51.5 0.4 multiply_reduce_fusion.7
  52.0 0.1 constant_dynamic-slice_fusion.4
  52.1 0.1 dynamic_slice.52
  52.2 0.1 dynamic_slice.53
  52.2 0.4 multiply_reduce_fusion.7
  52.7 0.1 constant_dynamic-slice_fusion.4
  52.8 0.1 dynamic_slice.52
  52.9 0.1 dynamic_slice.53
  52.9 0.4 multiply_reduce_fusion.7
  53.4 0.1 constant_dynamic-slice_fusion.4
  53.5 0.1 dynamic_slice.52
  53.6 0.1 dynamic_slice.53
  53.7 0.4 multiply_reduce_fusion.7
  54.1 0.0 collective-permute-done
  54.1 0.0 collective-permute-done.1
  54.2 65.3 %gather_fusion.1 = f32[16384]{0:T(1024)S(1)} fusion(f32[768]{0:T(1024)S(1)} %pad_maximum_fusion.2, s32[16384]{0:T(1024)S(1)} %broadcast_clamp_fusion), kind=kCustom, calls=%fused_computation.1 | custom fusion | bytes 196608 | tf_op jit(solution)/shard_map/gather | solution.py:70
  119.4 0.0 copy-start.2
  119.5 0.8 copy-done.2
  120.3 3.5 %gather_fusion.2 = f32[512]{0:T(512)S(1)} fusion(f32[256]{0:T(256)S(1)} %fusion.5, s32[1024]{0:T(1024)S(1)} %pad_clamp_fusion), kind=kCustom, calls=%fused_computation.2 | custom fusion | bytes 6144 | tf_op jit(solution)/shard_map/gather | solution.py:56
  123.9 1.9 collective-permute-start.2
  125.8 7.9 %collective-permute-start.3 = (f32[256]{0:T(256)S(1)}, f32[256]{0:T(256)S(1)}, u32[]{:S(2)}, u32[]{:S(2)}) collective-permute-start(f32[256]{0:T(256)S(1)} %get-tuple-element.359), channel_id=1, source_target_pairs={{8,0},{16,8},{24,16},{32,24},{40,32},{48,40},{56,48},{64,56},{72,6... | collective-permute-start | bytes 3080 | tf_op jit(solution)/shard_map/ppermute | solution.py:20
  133.7 1.2 collective-permute-done.3
  134.9 65.3 %gather_fusion.3 = f32[16384]{0:T(1024)S(1)} fusion(f32[768]{0:T(1024)S(1)} %pad_maximum_fusion.3, s32[16384]{0:T(1024)S(1)} %broadcast_clamp_fusion), kind=kCustom, calls=%fused_computation.3 | custom fusion | bytes 196608 | tf_op jit(solution)/shard_map/gather | solution.py:70
  200.3 0.0 copy-start.1
  200.3 28.3 %all_gather.7 = f32[5,2048]{1,0:T(8,128)S(1)} all-gather(f32[5,256]{1,0:T(8,128)S(1)} %fusion.3), channel_id=1, replica_groups=mesh['wide'=64,'narrow'=8] {'narrow'}, dimensions={1}, use_global_device_ids=true | all-gather | bytes 46080 | tf_op jit(solution)/shard_map/all_gather | solution.py:63
  228.6 3.5 %gather_fusion.4 = f32[512]{0:T(512)S(1)} fusion(f32[256]{0:T(256)S(1)} %multiply_add_fusion, s32[1024]{0:T(1024)S(1)} %pad_clamp_fusion), kind=kCustom, calls=%fused_computation.4 | custom fusion | bytes 6144 | tf_op jit(solution)/shard_map/gather | solution.py:56
  232.1 1.9 collective-permute-start.4
  234.0 7.9 %collective-permute-start.5 = (f32[256]{0:T(256)S(1)}, f32[256]{0:T(256)S(1)}, u32[]{:S(2)}, u32[]{:S(2)}) collective-permute-start(f32[256]{0:T(256)S(1)} %get-tuple-element.357), channel_id=1, source_target_pairs={{8,0},{16,8},{24,16},{32,24},{40,32},{48,40},{56,48},{64,56},{72,6... | collective-permute-start | bytes 3080 | tf_op jit(solution)/shard_map/ppermute | solution.py:20
  241.9 2.8 while.33
  241.9 0.1 constant_dynamic-slice_fusion.5
  242.0 0.1 dynamic_slice.54
  242.1 0.1 dynamic_slice.55
  242.2 0.4 multiply_reduce_fusion.8
  242.6 0.1 constant_dynamic-slice_fusion.5
  242.7 0.1 dynamic_slice.54
  242.8 0.1 dynamic_slice.55
  242.9 0.4 multiply_reduce_fusion.8
  243.4 0.1 constant_dynamic-slice_fusion.5
  243.4 0.1 dynamic_slice.54
  243.5 0.1 dynamic_slice.55
  243.6 0.4 multiply_reduce_fusion.8
  244.1 0.1 constant_dynamic-slice_fusion.5
  244.2 0.1 dynamic_slice.54
  244.2 0.1 dynamic_slice.55
  244.3 0.4 multiply_reduce_fusion.8
  244.8 65.3 %gather_fusion.5 = f32[16384]{0:T(1024)S(1)} fusion(f32[768]{0:T(1024)S(1)} %pad_maximum_fusion.4, s32[16384]{0:T(1024)S(1)} %broadcast_clamp_fusion), kind=kCustom, calls=%fused_computation.5 | custom fusion | bytes 196608 | tf_op jit(solution)/shard_map/gather | solution.py:70
  310.1 0.6 fusion.7
  (52 shorter events, 0.5 us)
Async XLA Ops:
  1.4 0.7 copy-start
  5.6 15.1 %copy-start.3 = (f32[3,256]{1,0:T(4,128)S(1)}, f32[3,256]{1,0:T(4,128)}, u32[]{:S(2)}) copy-start(f32[3,256]{1,0:T(4,128)} %param.10) | copy-start | bytes 9220
  5.6 48.5 %collective-permute-start = (f32[256]{0:T(256)S(1)}, f32[256]{0:T(256)S(1)}, u32[]{:S(2)}, u32[]{:S(2)}) collective-permute-start(f32[256]{0:T(256)S(1)} %get-tuple-element.360), channel_id=1, source_target_pairs={{0,8},{8,16},{16,24},{24,32},{32,40},{40,48},{48,56},{56,64},{64,7... | collective-permute-start | bytes 3080 | tf_op jit(solution)/shard_map/ppermute | solution.py:18
  7.5 46.6 %collective-permute-start.1 = (f32[256]{0:T(256)S(1)}, f32[256]{0:T(256)S(1)}, u32[]{:S(2)}, u32[]{:S(2)}) collective-permute-start(f32[256]{0:T(256)S(1)} %get-tuple-element.361), channel_id=1, source_target_pairs={{8,0},{16,8},{24,16},{32,24},{40,32},{48,40},{56,48},{64,56},{72,6... | collective-permute-start | bytes 3080 | tf_op jit(solution)/shard_map/ppermute | solution.py:20
  20.7 0.7 copy-start.6
  49.7 0.6 copy-start.4
  49.7 0.9 copy-start.5
  50.5 0.7 slice-start
  119.4 0.8 copy-start.2
  123.9 9.8 %collective-permute-start.2 = (f32[256]{0:T(256)S(1)}, f32[256]{0:T(256)S(1)}, u32[]{:S(2)}, u32[]{:S(2)}) collective-permute-start(f32[256]{0:T(256)S(1)} %get-tuple-element.358), channel_id=1, source_target_pairs={{0,8},{8,16},{16,24},{24,32},{32,40},{40,48},{48,56},{56,64},{64,7... | collective-permute-start | bytes 3080 | tf_op jit(solution)/shard_map/ppermute | solution.py:18
  125.8 9.1 %collective-permute-start.3 = (f32[256]{0:T(256)S(1)}, f32[256]{0:T(256)S(1)}, u32[]{:S(2)}, u32[]{:S(2)}) collective-permute-start(f32[256]{0:T(256)S(1)} %get-tuple-element.359), channel_id=1, source_target_pairs={{8,0},{16,8},{24,16},{32,24},{40,32},{48,40},{56,48},{64,56},{72,6... | collective-permute-start | bytes 3080 | tf_op jit(solution)/shard_map/ppermute | solution.py:20
  200.3 109.9 %copy-start.1 = (f32[256]{0:T(256)}, f32[256]{0:T(256)S(1)}, u32[]{:S(2)}) copy-start(f32[256]{0:T(256)S(1)} %multiply_add_fusion) | copy-start | bytes 3076
  232.1 12.7 %collective-permute-start.4 = (f32[256]{0:T(256)S(1)}, f32[256]{0:T(256)S(1)}, u32[]{:S(2)}, u32[]{:S(2)}) collective-permute-start(f32[256]{0:T(256)S(1)} %get-tuple-element.356), channel_id=1, source_target_pairs={{0,8},{8,16},{16,24},{24,32},{32,40},{40,48},{48,56},{56,64},{64,7... | collective-permute-start | bytes 3080 | tf_op jit(solution)/shard_map/ppermute | solution.py:18
  234.0 10.7 %collective-permute-start.5 = (f32[256]{0:T(256)S(1)}, f32[256]{0:T(256)S(1)}, u32[]{:S(2)}, u32[]{:S(2)}) collective-permute-start(f32[256]{0:T(256)S(1)} %get-tuple-element.357), channel_id=1, source_target_pairs={{8,0},{16,8},{24,16},{32,24},{40,32},{48,40},{56,48},{64,56},{72,6... | collective-permute-start | bytes 3080 | tf_op jit(solution)/shard_map/ppermute | solution.py:20
where the time goes:
time: 311 us
  local copies, waits for them, and re-layouts  213 us (68%)
  blocking collectives  56.5 us (18%)
  starting transfers between devices  34.7 us (11%)
  other arithmetic  4.31 us (1%)
    gather x6, local copies, waits for them, and re-layouts, laplace(): neighbour_vals = extended[stencil_slots]  196 us
    all_gather x2, blocking collectives, kernel_totals(): part_rows = lax.all_gather(stacked, 'narrow', axis=1, tiled=True)  56.5 us
    ppermute x3, starting transfers between devices, padded(): lax.ppermute(head, axis, [((i + 1) % count, i) for i in range(count)])  28.9 us
    gather x3, local copies, waits for them, and re-layouts, extend(): rim_values = padded(field_now[packet_rows], (('wide', 0),), send_len)  10.5 us
  transfers between devices with their start and end apart: 6, of which 1 were waited for; matrix products, arithmetic and copies ran while one was open for 2% of the time, Pallas kernels for 0%

commit v1 on v0

v1 whole, which is shorter than its diff:
```python
import functools
import jax
import jax.numpy as jnp
from jax import lax
from jax.experimental import pallas as pl
from jax.experimental.pallas import tpu as pltpu
from jax.sharding import PartitionSpec as P

kernel_strength = 0.1
gradient_energy = 0.5
time_step = 0.2

LANES = 128
MESH = pl.DeviceIdType.MESH
PEERS = ((0, 1), (1, 0), (3, 0), (1, 1), (3, 1), (2, 0), (2, 1))
CHUNK = 64


def halves(row):
    return row[:, :LANES], row[:, LANES:]


def lookup(row, lanes):
    return jnp.take_along_axis(
        jnp.broadcast_to(row, lanes.shape), lanes, axis=1, mode="promise_in_bounds"
    )


def step_kernel(
    n_wide, kernel_decay,
    pos_h, vol_h, field_h, weight_h, slot_h, list_h,
    next_o, pot_o,
    pos_v, vol_v, field_v, weight_v, slot_v, list_v,
    pack_s, pack_r, column, gauss, mass_acc, field_acc, masked, lane_of, pick,
    halo_s, halo_r, next_s, next_r,
    load_sem, pack_ss, pack_rs, halo_ss, halo_rs, next_ss, next_rs,
):
    wide = lax.axis_index("wide")
    narrow = lax.axis_index("narrow")
    x_at, y_at = narrow // 2, narrow % 2
    peers = [
        (wide, lax.rem(x_at + dx, 4) * 2 + lax.rem(y_at + dy, 2)) for dx, dy in PEERS
    ]
    up = (lax.rem(wide + 1, n_wide), narrow)
    down = (lax.rem(wide + n_wide - 1, n_wide), narrow)

    barrier = pltpu.get_barrier_semaphore()
    for target in (up, down, *reversed(peers)):
        pl.semaphore_signal(barrier, inc=1, device_id=target, device_id_type=MESH)

    loads = [
        pltpu.make_async_copy(src, dst, load_sem.at[i])
        for i, (src, dst) in enumerate(
            (
                (list_h, list_v), (field_h, field_v), (pos_h, pos_v), (vol_h, vol_v),
                (slot_h, slot_v), (weight_h, weight_v),
            )
        )
    ]
    for load in loads:
        load.start()

    def to_halo(rows, turn):
        low, high = halves(rows)
        pairs = pick[...]
        lanes = pairs & (LANES - 1)
        values = jnp.where(pairs >= LANES, lookup(high, lanes), lookup(low, lanes))
        halo_s[turn] = values[:4]

    def halo_copies(turn):
        return [
            pltpu.make_async_remote_copy(
                src_ref=halo_s.at[turn],
                dst_ref=halo_r.at[turn, side],
                send_sem=halo_ss.at[turn, side],
                recv_sem=halo_rs.at[turn, side],
                device_id=target,
                device_id_type=MESH,
            )
            for side, target in enumerate((up, down))
        ]

    def lap_part(rows, first, field_row):
        field_halves = halves(field_row)
        parts = []
        for at in range(2):
            lanes = lane_of[:, at * LANES:(at + 1) * LANES]
            total = None
            for h, row in enumerate(rows):
                weights = masked[first + h, :, at * LANES:(at + 1) * LANES]
                term = weights * (lookup(row, lanes) - field_halves[at])
                total = term if total is None else total + term
            parts.append(jnp.sum(total.reshape(8, 8, LANES), axis=0))
        return parts

    def halo_rows(turn, side):
        base = 2 * side
        return (
            halo_r[turn, side, base:base + 1, :],
            halo_r[turn, side, base + 1:base + 2, :],
        )

    def finish_lap(parts):
        return jnp.concatenate(
            [jnp.sum(part, axis=0, keepdims=True) for part in parts], axis=1
        )

    def lap_rest(parts, turn, field_row):
        copies = halo_copies(turn)
        for side in range(2):
            copies[side].wait_recv()
            more = lap_part(halo_rows(turn, side), 2 + 2 * side, field_row)
            parts = [a + b for a, b in zip(parts, more)]
        return finish_lap(parts)

    def add_sources(slot, source):
        rows = [source[r] for r in range(5)]
        for at in range(2):
            sx, sy, sz, sv, sf = [
                row[:, at * LANES:(at + 1) * LANES] for row in rows
            ]
            for t in range(0, 256, CHUNK):
                span = slice(t, t + CHUNK)
                distance = (column[0, span] - sx) ** 2
                distance = distance + (column[1, span] - sy) ** 2
                distance = distance + (column[2, span] - sz) ** 2
                value = jnp.exp(-kernel_decay * distance) * sv
                gauss[slot, at, span] = value
                if slot == 7 and at == 0:
                    mass_acc[span] = value
                    field_acc[span] = value * sf
                else:
                    mass_acc[span] += value
                    field_acc[span] += value * sf

    def add_field(slot, row):
        for at, part in enumerate(halves(row)):
            for t in range(0, 256, CHUNK):
                span = slice(t, t + CHUNK)
                value = gauss[slot, at, span] * part
                if slot == 7 and at == 0:
                    field_acc[span] = value
                else:
                    field_acc[span] += value

    def to_row(acc):
        return jnp.concatenate(
            [
                jnp.sum(acc[at * LANES:(at + 1) * LANES].T, axis=0, keepdims=True)
                for at in range(2)
            ],
            axis=1,
        )

    def potential(rows, mass, smooth, lap):
        kernel_term = mass * rows - kernel_strength * smooth
        return rows * rows * rows - rows + kernel_term - gradient_energy * lap

    loads[0].wait()
    loads[1].wait()
    for r in range(2):
        for at in range(2):
            pick[2 * r + at:2 * r + at + 1] = list_v[r:r + 1, at * LANES:(at + 1) * LANES]
    pick[4:8] = jnp.zeros((4, LANES), jnp.int32)
    field = field_v[...]
    to_halo(field, 0)
    loads[2].wait()
    loads[3].wait()
    for r in range(3):
        pack_s[r] = pos_v[r:r + 1]
    pack_s[3] = vol_v[...]
    pack_s[4] = field

    pl.semaphore_wait(barrier, 2 + len(peers))

    pack_copies = [
        pltpu.make_async_remote_copy(
            src_ref=pack_s,
            dst_ref=pack_r.at[i],
            send_sem=pack_ss.at[i],
            recv_sem=pack_rs.at[i],
            device_id=target,
            device_id_type=MESH,
        )
        for i, target in enumerate(peers)
    ]
    next_copies = [
        pltpu.make_async_remote_copy(
            src_ref=next_s,
            dst_ref=next_r.at[i],
            send_sem=next_ss.at[i],
            recv_sem=next_rs.at[i],
            device_id=target,
            device_id_type=MESH,
        )
        for i, target in enumerate(peers)
    ]
    for copy in halo_copies(0):
        copy.start()
    for copy in reversed(pack_copies):
        copy.start()

    for r in range(3):
        for at, part in enumerate(halves(pos_v[r:r + 1])):
            column[r, at * LANES:(at + 1) * LANES] = jnp.broadcast_to(part, (LANES, LANES)).T
    loads[4].wait()
    loads[5].wait()
    slots = slot_v[...]
    lane_of[...] = slots & (LANES - 1)
    rows_of = slots >> 7
    weights = weight_v[...]
    for h in range(6):
        masked[h] = jnp.where(rows_of == h, weights, 0.0)
    lap_now = lap_part(halves(field), 0, field)
    add_sources(7, pack_s)
    for i, copy in enumerate(pack_copies):
        copy.wait_recv()
        add_sources(i, pack_r.at[i])
    mass = kernel_strength * to_row(mass_acc[...])
    smooth = to_row(field_acc[...])
    lap = lap_rest(lap_now, 0, field)
    now = potential(field, mass, smooth, lap)

    to_halo(now, 1)
    for copy in halo_copies(1):
        copy.start()
    lap = lap_rest(lap_part(halves(now), 0, now), 1, now)
    after = field + time_step * lap

    next_s[...] = after
    to_halo(after, 2)
    for copy in halo_copies(2):
        copy.start()
    for copy in reversed(next_copies):
        copy.start()
    next_o[...] = after
    lap_own = lap_part(halves(after), 0, after)
    add_field(7, after)
    for i, copy in enumerate(next_copies):
        copy.wait_recv()
        add_field(i, next_r[i])
    smooth = to_row(field_acc[...])
    lap = lap_rest(lap_own, 2, after)
    pot_o[...] = potential(after, mass, smooth, lap)

    for copy in pack_copies + next_copies:
        copy.wait_send()
    for turn in range(3):
        for copy in halo_copies(turn):
            copy.wait_send()


def shards(n_wide, positions, volumes, phase_field, stencil_weights, stencil_slots, send_lists):
    own = phase_field.shape[0]
    patch_len = own * lax.axis_size("narrow")
    kernel_decay = 0.5 * float(patch_len) ** (2.0 / 3.0)
    row = jax.ShapeDtypeStruct((1, own), jnp.float32)
    in_hbm = pl.BlockSpec(memory_space=pl.ANY)
    in_vmem = pl.BlockSpec(memory_space=pltpu.VMEM)
    f32 = jnp.float32
    n_peers = len(PEERS)
    after, pot = pl.pallas_call(
        functools.partial(step_kernel, n_wide, kernel_decay),
        out_shape=(row, row),
        in_specs=[in_hbm] * 6,
        out_specs=(in_vmem, in_vmem),
        scratch_shapes=[
            pltpu.VMEM((3, own), f32),
            pltpu.VMEM((1, own), f32),
            pltpu.VMEM((1, own), f32),
            pltpu.VMEM(stencil_weights.shape, f32),
            pltpu.VMEM(stencil_slots.shape, jnp.int32),
            pltpu.VMEM((2, own), jnp.int32),
            pltpu.VMEM((5, 1, own), f32),
            pltpu.VMEM((n_peers, 5, 1, own), f32),
            pltpu.VMEM((3, own, LANES), f32),
            pltpu.VMEM((n_peers + 1, 2, own, LANES), f32),
            pltpu.VMEM((own, LANES), f32),
            pltpu.VMEM((own, LANES), f32),
            pltpu.VMEM((6, *stencil_weights.shape), f32),
            pltpu.VMEM(stencil_slots.shape, jnp.int32),
            pltpu.VMEM((8, LANES), jnp.int32),
            pltpu.VMEM((3, 4, LANES), f32),
            pltpu.VMEM((3, 2, 4, LANES), f32),
            pltpu.VMEM((1, own), f32),
            pltpu.VMEM((n_peers, 1, own), f32),
            pltpu.SemaphoreType.DMA((6,)),
            pltpu.SemaphoreType.DMA((n_peers,)),
            pltpu.SemaphoreType.DMA((n_peers,)),
            pltpu.SemaphoreType.DMA((3, 2)),
            pltpu.SemaphoreType.DMA((3, 2)),
            pltpu.SemaphoreType.DMA((n_peers,)),
            pltpu.SemaphoreType.DMA((n_peers,)),
        ],
        compiler_params=pltpu.CompilerParams(collective_id=0, has_side_effects=True),
    )(
        positions,
        volumes.reshape(1, own),
        phase_field.reshape(1, own),
        stencil_weights,
        stencil_slots,
        send_lists,
    )
    return after.reshape(own), pot.reshape(own)


def solution(mesh):
    placed = (
        P(None, ("wide", "narrow")),
        P(("wide", "narrow")),
        P(("wide", "narrow")),
        P(None, ("wide", "narrow")),
        P(None, ("wide", "narrow")),
        P(None, ("wide", "narrow")),
    )
    return jax.shard_map(
        functools.partial(shards, mesh.shape["wide"]),
        mesh=mesh,
        in_specs=placed,
        out_specs=(P(("wide", "narrow")), P(("wide", "narrow"))),
        check_vma=False,
    )
```

time: 311 us -> 31.1 us (0.10)
  the two profiles are of different devices: /device:TPU:14 before, /device:TPU:8 now
where the time goes in v1:
time: 31.1 us; the launch traced here: 30.9 us
  Pallas kernels  28.4 us (91%)
  local copies, waits for them, and re-layouts  1.86 us (6%)
  between operations  0.65 us (2%)
    pallas_call x1, Pallas kernels, shards(): pl.pallas_call(functools.partial(step_kernel, n_wide, kernel_decay), out_...  28.4 us
    unnamed x6, local copies, waits for them, and re-layouts  1.86 us

profile of v1, /device:TPU:8, one launch (start us, length us, event | category | flops | bytes accessed | tf_op | source)
XLA Modules:
  0.0 30.9 jit_solution(5583717035384631148)
XLA Ops:
  0.6 28.4 %shard_map.77 = (f32[1,256]{1,0:T(1,128)}, f32[1,256]{1,0:T(1,128)}) custom-call(f32[3,256]{1,0:T(4,128)} %pos_h.1, f32[1,256]{1,0:T(1,128)} %bitcast.4, f32[1,256]{1,0:T(1,128)} %bitcast.5, f32[64,256]{1,0:T(8,128)} %weight_h.1, s32[64,256]{1,0:T(8,128)} %slot_h.1, s32[2,256]{1,0:T(2,128)} %list_h.1), custom_call_target="tpu_custom_call" | custom-call | tf_op jit(solution)/shard_map/pallas_call | solution.py:262
  29.0 0.0 copy-start.1
  29.0 0.7 %copy-done.1 = f32[1,256]{1,0:T(1,128)S(1)} copy-done((f32[1,256]{1,0:T(1,128)S(1)}, f32[1,256]{1,0:T(1,128)}, u32[]{:S(2)}) %copy-start.1) | copy-done | bytes 1048
  29.7 0.0 copy-start
  29.7 0.6 %copy.10 = f32[256]{0:T(256)} copy(f32[256]{0:T(256)S(1)} %bitcast.7) | data formatting | bytes 2048
  30.3 0.1 copy-done
  30.3 0.6 %copy.11 = f32[256]{0:T(256)} copy(f32[256]{0:T(256)S(1)} %bitcast.6) | data formatting | bytes 2048
Async XLA Ops:
  29.0 0.7 %copy-start.1 = (f32[1,256]{1,0:T(1,128)S(1)}, f32[1,256]{1,0:T(1,128)}, u32[]{:S(2)}) copy-start(f32[1,256]{1,0:T(1,128)} %get-tuple-element.4) | copy-start | bytes 3076
  29.7 0.6 %copy-start = (f32[1,256]{1,0:T(1,128)S(1)}, f32[1,256]{1,0:T(1,128)}, u32[]{:S(2)}) copy-start(f32[1,256]{1,0:T(1,128)} %get-tuple-element.5) | copy-start | bytes 3076

commit v2 on v1

--- a/solution.py
+++ b/solution.py
@@ -29,7 +29,7 @@
 def step_kernel(
     n_wide, kernel_decay,
     pos_h, vol_h, field_h, weight_h, slot_h, list_h,
-    next_o, pot_o,
+    out_o,
     pos_v, vol_v, field_v, weight_v, slot_v, list_v,
     pack_s, pack_r, column, gauss, mass_acc, field_acc, masked, lane_of, pick,
     halo_s, halo_r, next_s, next_r,
@@ -233,7 +233,7 @@
         copy.start()
     for copy in reversed(next_copies):
         copy.start()
-    next_o[...] = after
+    out_o[0] = after
     lap_own = lap_part(halves(after), 0, after)
     add_field(7, after)
     for i, copy in enumerate(next_copies):
@@ -241,7 +241,7 @@
         add_field(i, next_r[i])
     smooth = to_row(field_acc[...])
     lap = lap_rest(lap_own, 2, after)
-    pot_o[...] = potential(after, mass, smooth, lap)
+    out_o[1] = potential(after, mass, smooth, lap)
 
     for copy in pack_copies + next_copies:
         copy.wait_send()
@@ -254,16 +254,15 @@
     own = phase_field.shape[0]
     patch_len = own * lax.axis_size("narrow")
     kernel_decay = 0.5 * float(patch_len) ** (2.0 / 3.0)
-    row = jax.ShapeDtypeStruct((1, own), jnp.float32)
-    in_hbm = pl.BlockSpec(memory_space=pl.ANY)
+    in_hbm = pl.BlockSpec(memory_space=pltpu.HBM)
     in_vmem = pl.BlockSpec(memory_space=pltpu.VMEM)
     f32 = jnp.float32
     n_peers = len(PEERS)
-    after, pot = pl.pallas_call(
+    both = pl.pallas_call(
         functools.partial(step_kernel, n_wide, kernel_decay),
-        out_shape=(row, row),
+        out_shape=jax.ShapeDtypeStruct((2, 1, own), f32),
         in_specs=[in_hbm] * 6,
-        out_specs=(in_vmem, in_vmem),
+        out_specs=in_vmem,
         scratch_shapes=[
             pltpu.VMEM((3, own), f32),
             pltpu.VMEM((1, own), f32),
@@ -292,16 +291,24 @@
             pltpu.SemaphoreType.DMA((n_peers,)),
             pltpu.SemaphoreType.DMA((n_peers,)),
         ],
-        compiler_params=pltpu.CompilerParams(collective_id=0, has_side_effects=True),
+        compiler_params=pltpu.CompilerParams(
+            collective_id=0, has_side_effects=True, vmem_limit_bytes=16 * 1024 * 1024
+        ),
     )(
-        positions,
-        volumes.reshape(1, own),
-        phase_field.reshape(1, own),
-        stencil_weights,
-        stencil_slots,
-        send_lists,
+        *(
+            pltpu.with_memory_space_constraint(array, pltpu.HBM)
+            for array in (
+                positions,
+                volumes.reshape(1, own),
+                phase_field.reshape(1, own),
+                stencil_weights,
+                stencil_slots,
+                send_lists,
+            )
+        )
     )
-    return after.reshape(own), pot.reshape(own)
+    both = both.reshape(2 * own)
+    return both[:own], both[own:]
 
 
 def solution(mesh):

time: 31.1 us -> 29.2 us (0.939)
  local copies, waits for them, and re-layouts: 1.86 us -> 0.57 us
  Pallas kernels: 28.4 us -> 27.8 us
    unnamed x6 -> x0, local copies, waits for them, and re-layouts: 1.86 us -> none
    pallas_call x1, Pallas kernels: 28.4 us -> 27.8 us  [shards(): pl.pallas_call(functools.partial(step_kernel, n_wide, kernel_decay), out_...]
    slice x0 -> x1, local copies, waits for them, and re-layouts: none -> 0.57 us  [shards(): return (both[:own], both[own:])]
where the time goes in v2:
time: 29.2 us; the launch traced here: 29 us
  Pallas kernels  27.8 us (95%)
  between operations  0.64 us (2%)
  local copies, waits for them, and re-layouts  0.57 us (2%)
    pallas_call x1, Pallas kernels, shards(): pl.pallas_call(functools.partial(step_kernel, n_wide, kernel_decay), out_...  27.8 us

profile of v2, /device:TPU:8, one launch (start us, length us, event | category | flops | bytes accessed | tf_op | source)
XLA Modules:
  0.0 29.0 jit_solution(1777357146254454089)
XLA Ops:
  0.6 27.8 %shard_map.77 = f32[2,1,256]{2,1,0:T(1,128)S(1)} custom-call(f32[3,256]{1,0:T(4,128)} %pos_h.1, f32[1,256]{1,0:T(1,128)} %bitcast.4, f32[1,256]{1,0:T(1,128)} %bitcast.5, f32[64,256]{1,0:T(8,128)} %weight_h.1, s32[64,256]{1,0:T(8,128)} %slot_h.1, s32[2,256]{1,0:T(2,128)} %list_h.1), custom_call_target="tpu_custom_call" | custom-call | tf_op jit(solution)/shard_map/pallas_call | solution.py:261
  28.4 0.6 %fusion = (f32[1,1,256]{2,1,0:T(1,128)}, f32[1,1,256]{2,1,0:T(1,128)}) fusion(f32[2,1,256]{2,1,0:T(1,128)S(1)} %shard_map.77), kind=kLoop, calls=%fused_computation | loop fusion | bytes 4096 | tf_op jit(solution)/shard_map/slice | solution.py:311

commit v3 on v2

v3 whole, which is shorter than its diff:
```python
import functools
import jax
import jax.numpy as jnp
from jax import lax
from jax.experimental import pallas as pl
from jax.experimental.pallas import tpu as pltpu
from jax.sharding import PartitionSpec as P

kernel_strength = 0.1
gradient_energy = 0.5
time_step = 0.2

LANES = 128
MESH = pl.DeviceIdType.MESH
PEERS = ((0, 1), (1, 0), (3, 0), (1, 1), (3, 1), (2, 0), (2, 1))
CHUNK = 64
LOG2_E = 1.4426950408889634


def halves(row):
    return row[:, :LANES], row[:, LANES:]


def lookup(row, lanes):
    return jnp.take_along_axis(
        jnp.broadcast_to(row, lanes.shape), lanes, axis=1, mode="promise_in_bounds"
    )


def join(pair):
    return jnp.concatenate(pair, axis=1)


def step_kernel(
    n_wide, kernel_decay,
    pos_h, vol_h, field_h, weight_h, slot_h, list_h,
    out_o,
    pos_v, vol_v, field_v, weight_v, slot_v, list_v,
    pack_s, pack_r, column, gauss, acc, masked, lane_of, pick,
    halo_s, halo_r, next_s, next_r,
    load_sem, send_sem, pack_rs, halo_rs, next_rs,
):
    wide = lax.axis_index("wide")
    narrow = lax.axis_index("narrow")
    x_at, y_at = narrow // 2, narrow % 2
    peers = [
        (wide, lax.rem(x_at + dx, 4) * 2 + lax.rem(y_at + dy, 2)) for dx, dy in PEERS
    ]
    up = (lax.rem(wide + 1, n_wide), narrow)
    down = (lax.rem(wide + n_wide - 1, n_wide), narrow)
    near_side = 1 - wide % 2
    far_side = 1 - near_side

    barrier = pltpu.get_barrier_semaphore()
    for target in (up, down, *reversed(peers)):
        pl.semaphore_signal(barrier, inc=1, device_id=target, device_id_type=MESH)

    loads = [
        pltpu.make_async_copy(src, dst, load_sem.at[i])
        for i, (src, dst) in enumerate(
            (
                (list_h, list_v), (field_h, field_v), (pos_h, pos_v), (vol_h, vol_v),
                (slot_h, slot_v), (weight_h, weight_v),
            )
        )
    ]
    for load in loads:
        load.start()

    def to_halo(rows, turn):
        low, high = halves(rows)
        pairs = pick[...]
        lanes = pairs & (LANES - 1)
        values = jnp.where(pairs >= LANES, lookup(high, lanes), lookup(low, lanes))
        halo_s[turn] = values[:4]

    def halo_copies(turn):
        return [
            pltpu.make_async_remote_copy(
                src_ref=halo_s.at[turn],
                dst_ref=halo_r.at[turn, side],
                send_sem=send_sem.at[1],
                recv_sem=halo_rs.at[turn, side],
                device_id=target,
                device_id_type=MESH,
            )
            for side, target in enumerate((up, down))
        ]

    def halo_wait(turn, side):
        pltpu.make_async_remote_copy(
            src_ref=halo_s.at[turn],
            dst_ref=halo_r.at[turn, side],
            send_sem=send_sem.at[1],
            recv_sem=halo_rs.at[turn, side],
            device_id=up,
            device_id_type=MESH,
        ).wait_recv()

    def lap_part(rows, first, field_row):
        field_halves = halves(field_row)
        parts = []
        for at in range(2):
            lanes = lane_of[:, at * LANES:(at + 1) * LANES]
            total = None
            for h, row in enumerate(rows):
                weights = masked[first, h, :, at * LANES:(at + 1) * LANES]
                term = weights * (lookup(row, lanes) - field_halves[at])
                total = term if total is None else total + term
            parts.append(jnp.sum(total.reshape(8, 8, LANES), axis=0))
        return parts

    def lap_side(parts, turn, side, field_row):
        halo_wait(turn, side)
        rows = halo_r[turn, side]
        is_high = side == 1
        rows = [jnp.where(is_high, rows[2 + h:3 + h], rows[h:h + 1]) for h in range(2)]
        more = lap_part(rows, 1 + side, field_row)
        return [a + b for a, b in zip(parts, more)]

    def add_sources(slot, source):
        rows = [halves(source[r]) for r in range(5)]
        for t in range(0, 256, CHUNK):
            span = slice(t, t + CHUNK)
            total = None
            for at in range(2):
                sx, sy, sz, sv, sf = [row[at] for row in rows]
                distance = (column[0, span] - sx) ** 2
                distance = distance + (column[1, span] - sy) ** 2
                distance = distance + (column[2, span] - sz) ** 2
                value = jnp.exp2(distance * (-kernel_decay * LOG2_E)) * sv
                gauss[slot, at, span] = value
                term = value * (column[3, span] - sf)
                total = term if total is None else total + term
            if slot == 7:
                acc[span] = total
            else:
                acc[span] += total

    def add_field(slot, row):
        low, high = halves(row)
        for t in range(0, 256, CHUNK):
            span = slice(t, t + CHUNK)
            value = gauss[slot, 0, span] * low + gauss[slot, 1, span] * high
            if slot == 7:
                acc[span] = value
            else:
                acc[span] += value

    def fold(total):
        return [
            jnp.sum(total[at * LANES:(at + 1) * LANES].T.reshape(16, 8, LANES), axis=0)
            for at in range(2)
        ]

    def finish(parts):
        return join([jnp.sum(part, axis=0, keepdims=True) for part in parts])

    loads[0].wait()
    loads[1].wait()
    for r in range(2):
        for at in range(2):
            pick[2 * r + at:2 * r + at + 1] = list_v[r:r + 1, at * LANES:(at + 1) * LANES]
    pick[4:8] = jnp.zeros((4, LANES), jnp.int32)
    field = field_v[...]
    to_halo(field, 0)
    loads[2].wait()
    loads[3].wait()
    for r in range(3):
        pack_s[r] = pos_v[r:r + 1]
    pack_s[3] = vol_v[...]
    pack_s[4] = field

    pl.semaphore_wait(barrier, 2 + len(peers))

    pack_copies = [
        pltpu.make_async_remote_copy(
            src_ref=pack_s,
            dst_ref=pack_r.at[i],
            send_sem=send_sem.at[0],
            recv_sem=pack_rs.at[i],
            device_id=target,
            device_id_type=MESH,
        )
        for i, target in enumerate(peers)
    ]
    next_copies = [
        pltpu.make_async_remote_copy(
            src_ref=next_s,
            dst_ref=next_r.at[i],
            send_sem=send_sem.at[2],
            recv_sem=next_rs.at[i],
            device_id=target,
            device_id_type=MESH,
        )
        for i, target in enumerate(peers)
    ]
    for copy in halo_copies(0):
        copy.start()
    for copy in reversed(pack_copies):
        copy.start()

    for r, row in enumerate((pos_v[0:1], pos_v[1:2], pos_v[2:3], field)):
        for at, part in enumerate(halves(row)):
            column[r, at * LANES:(at + 1) * LANES] = jnp.broadcast_to(part, (LANES, LANES)).T
    add_sources(7, pack_s)
    loads[4].wait()
    loads[5].wait()
    slots = slot_v[...]
    lane_of[...] = slots & (LANES - 1)
    rows_of = slots >> 7
    weights = weight_v[...]
    for h in range(6):
        masked[h // 2, h % 2] = jnp.where(rows_of == h, weights, 0.0)
    lap = lap_part(halves(field), 0, field)
    for i in range(3):
        pack_copies[i].wait_recv()
        add_sources(i, pack_r.at[i])
    lap = lap_side(lap, 0, near_side, field)
    for i in range(3, 6):
        pack_copies[i].wait_recv()
        add_sources(i, pack_r.at[i])
    lap = lap_side(lap, 0, far_side, field)
    pack_copies[6].wait_recv()
    add_sources(6, pack_r.at[6])
    kernel_term = fold(acc[...])
    now = field * field * field - field + finish(
        [kernel_strength * a - gradient_energy * b for a, b in zip(kernel_term, lap)]
    )

    to_halo(now, 1)
    for copy in halo_copies(1):
        copy.start()
    lap = lap_part(halves(now), 0, now)
    lap = lap_side(lap, 1, near_side, now)
    for t in range(0, 256, CHUNK):
        span = slice(t, t + CHUNK)
        total = gauss[0, 0, span] + gauss[0, 1, span]
        for slot in range(1, 8):
            total = total + (gauss[slot, 0, span] + gauss[slot, 1, span])
        acc[span] = total
    mass = finish([kernel_strength * a for a in fold(acc[...])])
    after = field + time_step * finish(lap_side(lap, 1, far_side, now))

    next_s[...] = after
    for copy in reversed(next_copies):
        copy.start()
    to_halo(after, 2)
    for copy in halo_copies(2):
        copy.start()
    out_o[0] = after
    rest = after * after * after - after + mass * after
    lap = lap_part(halves(after), 0, after)
    add_field(7, after)
    for i in range(3):
        next_copies[i].wait_recv()
        add_field(i, next_r[i])
    lap = lap_side(lap, 2, near_side, after)
    for i in range(3, 6):
        next_copies[i].wait_recv()
        add_field(i, next_r[i])
    lap = lap_side(lap, 2, far_side, after)
    next_copies[6].wait_recv()
    add_field(6, next_r[6])
    smooth = fold(acc[...])
    out_o[1] = rest - finish(
        [kernel_strength * a + gradient_energy * b for a, b in zip(smooth, lap)]
    )

    for kind, whole in enumerate((pack_r, halo_r, next_r)):
        pltpu.make_async_copy(whole, whole, send_sem.at[kind]).wait()


def shards(n_wide, positions, volumes, phase_field, stencil_weights, stencil_slots, send_lists):
    own = phase_field.shape[0]
    patch_len = own * lax.axis_size("narrow")
    kernel_decay = 0.5 * float(patch_len) ** (2.0 / 3.0)
    in_hbm = pl.BlockSpec(memory_space=pltpu.HBM)
    in_vmem = pl.BlockSpec(memory_space=pltpu.VMEM)
    f32 = jnp.float32
    n_peers = len(PEERS)
    both = pl.pallas_call(
        functools.partial(step_kernel, n_wide, kernel_decay),
        out_shape=jax.ShapeDtypeStruct((2, 1, own), f32),
        in_specs=[in_hbm] * 6,
        out_specs=in_vmem,
        scratch_shapes=[
            pltpu.VMEM((3, own), f32),
            pltpu.VMEM((1, own), f32),
            pltpu.VMEM((1, own), f32),
            pltpu.VMEM(stencil_weights.shape, f32),
            pltpu.VMEM(stencil_slots.shape, jnp.int32),
            pltpu.VMEM((2, own), jnp.int32),
            pltpu.VMEM((5, 1, own), f32),
            pltpu.VMEM((n_peers, 5, 1, own), f32),
            pltpu.VMEM((4, own, LANES), f32),
            pltpu.VMEM((n_peers + 1, 2, own, LANES), f32),
            pltpu.VMEM((own, LANES), f32),
            pltpu.VMEM((3, 2, *stencil_weights.shape), f32),
            pltpu.VMEM(stencil_slots.shape, jnp.int32),
            pltpu.VMEM((8, LANES), jnp.int32),
            pltpu.VMEM((3, 4, LANES), f32),
            pltpu.VMEM((3, 2, 4, LANES), f32),
            pltpu.VMEM((1, own), f32),
            pltpu.VMEM((n_peers, 1, own), f32),
            pltpu.SemaphoreType.DMA((6,)),
            pltpu.SemaphoreType.DMA((3,)),
            pltpu.SemaphoreType.DMA((n_peers,)),
            pltpu.SemaphoreType.DMA((3, 2)),
            pltpu.SemaphoreType.DMA((n_peers,)),
        ],
        compiler_params=pltpu.CompilerParams(
            collective_id=0, has_side_effects=True, vmem_limit_bytes=16 * 1024 * 1024
        ),
    )(
        *(
            pltpu.with_memory_space_constraint(array, pltpu.HBM)
            for array in (
                positions,
                volumes.reshape(1, own),
                phase_field.reshape(1, own),
                stencil_weights,
                stencil_slots,
                send_lists,
            )
        )
    )
    both = both.reshape(2 * own)
    return both[:own], both[own:]


def solution(mesh):
    placed = (
        P(None, ("wide", "narrow")),
        P(("wide", "narrow")),
        P(("wide", "narrow")),
        P(None, ("wide", "narrow")),
        P(None, ("wide", "narrow")),
        P(None, ("wide", "narrow")),
    )
    return jax.shard_map(
        functools.partial(shards, mesh.shape["wide"]),
        mesh=mesh,
        in_specs=placed,
        out_specs=(P(("wide", "narrow")), P(("wide", "narrow"))),
        check_vma=False,
    )
```

time: 29.2 us -> 28.8 us (0.986)
  Pallas kernels: 27.8 us -> 27.4 us
    pallas_call x1, Pallas kernels: 27.8 us -> 27.4 us  [shards(): pl.pallas_call(functools.partial(step_kernel, n_wide, kernel_decay), out_...]
where the time goes in v3:
time: 28.8 us; the launch traced here: 28.6 us
  Pallas kernels  27.4 us (95%)
  between operations  0.64 us (2%)
  local copies, waits for them, and re-layouts  0.57 us (2%)
    pallas_call x1, Pallas kernels, shards(): pl.pallas_call(functools.partial(step_kernel, n_wide, kernel_decay), out_...  27.4 us

profile of v3, /device:TPU:8, one launch (start us, length us, event | category | flops | bytes accessed | tf_op | source)
XLA Modules:
  0.0 28.6 jit_solution(10968040398631896650)
XLA Ops:
  0.6 27.4 %shard_map.77 = f32[2,1,256]{2,1,0:T(1,128)S(1)} custom-call(f32[3,256]{1,0:T(4,128)} %pos_h.1, f32[1,256]{1,0:T(1,128)} %bitcast.4, f32[1,256]{1,0:T(1,128)} %bitcast.5, f32[64,256]{1,0:T(8,128)} %weight_h.1, s32[64,256]{1,0:T(8,128)} %slot_h.1, s32[2,256]{1,0:T(2,128)} %list_h.1), custom_call_target="tpu_custom_call" | custom-call | tf_op jit(solution)/shard_map/pallas_call | solution.py:282
  28.1 0.6 %fusion = (f32[1,1,256]{2,1,0:T(1,128)}, f32[1,1,256]{2,1,0:T(1,128)}) fusion(f32[2,1,256]{2,1,0:T(1,128)S(1)} %shard_map.77), kind=kLoop, calls=%fused_computation | loop fusion | bytes 4096 | tf_op jit(solution)/shard_map/slice | solution.py:329

commit v4 on v3

--- a/solution.py
+++ b/solution.py
@@ -38,7 +38,9 @@
     pos_v, vol_v, field_v, weight_v, slot_v, list_v,
     pack_s, pack_r, column, gauss, acc, masked, lane_of, pick,
     halo_s, halo_r, next_s, next_r,
-    load_sem, send_sem, pack_rs, halo_rs, next_rs,
+    edge_weight, edge_slot, edge_list, edge_field, edge_part, edge_halo,
+    edge_masked, edge_lane, edge_pick, edge_now, part_s,
+    load_sem, send_sem, pack_rs, halo_rs, next_rs, edge_rs,
 ):
     wide = lax.axis_index("wide")
     narrow = lax.axis_index("narrow")
@@ -50,6 +52,8 @@
     down = (lax.rem(wide + n_wide - 1, n_wide), narrow)
     near_side = 1 - wide % 2
     far_side = 1 - near_side
+    is_first, is_last, is_before = wide == 0, wide == n_wide - 1, wide == n_wide - 2
+    first = (0, narrow)
 
     barrier = pltpu.get_barrier_semaphore()
     for target in (up, down, *reversed(peers)):
@@ -67,12 +71,55 @@
     for load in loads:
         load.start()
 
+    def listed(rows, pairs):
+        low, high = halves(rows)
+        lanes = pairs & (LANES - 1)
+        return jnp.where(pairs >= LANES, lookup(high, lanes), lookup(low, lanes))
+
+    def set_pick(into, lists):
+        for r in range(2):
+            for at in range(2):
+                into[2 * r + at:2 * r + at + 1] = lists[r:r + 1, at * LANES:(at + 1) * LANES]
+        into[4:8] = jnp.zeros((4, LANES), jnp.int32)
+
+    def set_stencil(masked_ref, lane_ref, slots, weights):
+        lane_ref[...] = slots & (LANES - 1)
+        rows_of = slots >> 7
+        for h in range(6):
+            masked_ref[h // 2, h % 2] = jnp.where(rows_of == h, weights, 0.0)
+
     def to_halo(rows, turn):
-        low, high = halves(rows)
-        pairs = pick[...]
-        lanes = pairs & (LANES - 1)
-        values = jnp.where(pairs >= LANES, lookup(high, lanes), lookup(low, lanes))
-        halo_s[turn] = values[:4]
+        halo_s[turn] = listed(rows, pick[...])[:4]
+
+    def start_halo(turn):
+        copies = halo_copies(turn)
+        copies[1].start()
+        if turn == 0:
+            copies[0].start()
+        else:
+            @pl.when(jnp.logical_not(is_last))
+            def _():
+                copies[0].start()
+
+    def edge_copy(i, src, dst):
+        return pltpu.make_async_remote_copy(
+            src_ref=src,
+            dst_ref=dst,
+            send_sem=send_sem.at[3],
+            recv_sem=edge_rs.at[i],
+            device_id=first,
+            device_id_type=MESH,
+        )
+
+    edge_copies = [
+        edge_copy(i, src, dst)
+        for i, (src, dst) in enumerate(
+            (
+                (list_v, edge_list), (field_v, edge_field), (slot_v, edge_slot),
+                (weight_v, edge_weight), (part_s, edge_part), (halo_s.at[1], edge_halo),
+            )
+        )
+    ]
 
     def halo_copies(turn):
         return [
@@ -97,26 +144,27 @@
             device_id_type=MESH,
         ).wait_recv()
 
-    def lap_part(rows, first, field_row):
+    def lap_part(rows, kind, field_row, lane_ref=lane_of, masked_ref=masked):
         field_halves = halves(field_row)
         parts = []
         for at in range(2):
-            lanes = lane_of[:, at * LANES:(at + 1) * LANES]
+            lanes = lane_ref[:, at * LANES:(at + 1) * LANES]
             total = None
             for h, row in enumerate(rows):
-                weights = masked[first, h, :, at * LANES:(at + 1) * LANES]
+                weights = masked_ref[kind, h, :, at * LANES:(at + 1) * LANES]
                 term = weights * (lookup(row, lanes) - field_halves[at])
                 total = term if total is None else total + term
             parts.append(jnp.sum(total.reshape(8, 8, LANES), axis=0))
         return parts
 
-    def lap_side(parts, turn, side, field_row):
-        halo_wait(turn, side)
+    def lap_side(turn, side, field_row):
         rows = halo_r[turn, side]
         is_high = side == 1
         rows = [jnp.where(is_high, rows[2 + h:3 + h], rows[h:h + 1]) for h in range(2)]
-        more = lap_part(rows, 1 + side, field_row)
-        return [a + b for a, b in zip(parts, more)]
+        return lap_part(rows, 1 + side, field_row)
+
+    def add(*lists):
+        return [functools.reduce(jnp.add, parts) for parts in zip(*lists)]
 
     def add_sources(slot, source):
         rows = [halves(source[r]) for r in range(5)]
@@ -158,10 +206,7 @@
 
     loads[0].wait()
     loads[1].wait()
-    for r in range(2):
-        for at in range(2):
-            pick[2 * r + at:2 * r + at + 1] = list_v[r:r + 1, at * LANES:(at + 1) * LANES]
-    pick[4:8] = jnp.zeros((4, LANES), jnp.int32)
+    set_pick(pick, list_v[...])
     field = field_v[...]
     to_halo(field, 0)
     loads[2].wait()
@@ -195,44 +240,53 @@
         )
         for i, target in enumerate(peers)
     ]
-    for copy in halo_copies(0):
-        copy.start()
     for copy in reversed(pack_copies):
         copy.start()
+    start_halo(0)
+    loads[4].wait()
+    loads[5].wait()
+
+    @pl.when(is_last)
+    def _():
+        for i in range(4):
+            edge_copies[i].start()
 
     for r, row in enumerate((pos_v[0:1], pos_v[1:2], pos_v[2:3], field)):
         for at, part in enumerate(halves(row)):
             column[r, at * LANES:(at + 1) * LANES] = jnp.broadcast_to(part, (LANES, LANES)).T
     add_sources(7, pack_s)
-    loads[4].wait()
-    loads[5].wait()
-    slots = slot_v[...]
-    lane_of[...] = slots & (LANES - 1)
-    rows_of = slots >> 7
-    weights = weight_v[...]
-    for h in range(6):
-        masked[h // 2, h % 2] = jnp.where(rows_of == h, weights, 0.0)
+    set_stencil(masked, lane_of, slot_v[...], weight_v[...])
     lap = lap_part(halves(field), 0, field)
-    for i in range(3):
+    for i in range(5):
         pack_copies[i].wait_recv()
         add_sources(i, pack_r.at[i])
-    lap = lap_side(lap, 0, near_side, field)
-    for i in range(3, 6):
+    halo_wait(0, near_side)
+    lap = add(lap, lap_side(0, near_side, field))
+    for i in range(5, 7):
         pack_copies[i].wait_recv()
         add_sources(i, pack_r.at[i])
-    lap = lap_side(lap, 0, far_side, field)
-    pack_copies[6].wait_recv()
-    add_sources(6, pack_r.at[6])
-    kernel_term = fold(acc[...])
-    now = field * field * field - field + finish(
-        [kernel_strength * a - gradient_energy * b for a, b in zip(kernel_term, lap)]
-    )
+    part = field * field * field - field + finish(
+        [kernel_strength * a - gradient_energy * b for a, b in zip(fold(acc[...]), lap)]
+    )
+
+    @pl.when(is_last)
+    def _():
+        part_s[...] = part
+        edge_copies[4].start()
+
+    halo_wait(0, far_side)
+    now = part - gradient_energy * finish(lap_side(0, far_side, field))
 
     to_halo(now, 1)
-    for copy in halo_copies(1):
-        copy.start()
+    start_halo(1)
+
+    @pl.when(is_before)
+    def _():
+        edge_copies[5].start()
+
     lap = lap_part(halves(now), 0, now)
-    lap = lap_side(lap, 1, near_side, now)
+    halo_wait(1, near_side)
+    lap = add(lap, lap_side(1, near_side, now))
     for t in range(0, 256, CHUNK):
         span = slice(t, t + CHUNK)
         total = gauss[0, 0, span] + gauss[0, 1, span]
@@ -240,26 +294,67 @@
             total = total + (gauss[slot, 0, span] + gauss[slot, 1, span])
         acc[span] = total
     mass = finish([kernel_strength * a for a in fold(acc[...])])
-    after = field + time_step * finish(lap_side(lap, 1, far_side, now))
+
+    @pl.when(jnp.logical_not(is_first))
+    def _():
+        halo_wait(1, far_side)
+
+    @pl.when(is_first)
+    def _():
+        for i in range(4):
+            edge_copies[i].wait_recv()
+        set_pick(edge_pick, edge_list[...])
+        set_stencil(edge_masked, edge_lane, edge_slot[...], edge_weight[...])
+        theirs = edge_field[...]
+        rows = [halo_s[0, 2 + h:3 + h] for h in range(2)]
+        high = finish(lap_part(rows, 2, theirs, edge_lane, edge_masked))
+        edge_copies[4].wait_recv()
+        theirs_now = edge_part[...] - gradient_energy * high
+        edge_now[...] = theirs_now
+        halo_r[1, 0] = listed(theirs_now, edge_pick[...])[:4]
+
+    after = field + time_step * finish(add(lap, lap_side(1, far_side, now)))
 
     next_s[...] = after
     for copy in reversed(next_copies):
         copy.start()
     to_halo(after, 2)
-    for copy in halo_copies(2):
-        copy.start()
+    start_halo(2)
     out_o[0] = after
     rest = after * after * after - after + mass * after
     lap = lap_part(halves(after), 0, after)
     add_field(7, after)
+
+    @pl.when(is_first)
+    def _():
+        theirs_now = edge_now[...]
+        edge_copies[5].wait_recv()
+        rows = [
+            halves(theirs_now),
+            [edge_halo[h:h + 1] for h in range(2)],
+            [halo_s[1, 2 + h:3 + h] for h in range(2)],
+        ]
+        lap_next = add(*(
+            lap_part(pair, kind, theirs_now, edge_lane, edge_masked)
+            for kind, pair in enumerate(rows)
+        ))
+        theirs_after = edge_field[...] + time_step * finish(lap_next)
+        halo_r[2, 0] = listed(theirs_after, edge_pick[...])[:4]
+
     for i in range(3):
         next_copies[i].wait_recv()
         add_field(i, next_r[i])
-    lap = lap_side(lap, 2, near_side, after)
+    halo_wait(2, near_side)
+    lap = add(lap, lap_side(2, near_side, after))
     for i in range(3, 6):
         next_copies[i].wait_recv()
         add_field(i, next_r[i])
-    lap = lap_side(lap, 2, far_side, after)
+
+    @pl.when(jnp.logical_not(is_first))
+    def _():
+        halo_wait(2, far_side)
+
+    lap = add(lap, lap_side(2, far_side, after))
     next_copies[6].wait_recv()
     add_field(6, next_r[6])
     smooth = fold(acc[...])
@@ -267,8 +362,25 @@
         [kernel_strength * a + gradient_energy * b for a, b in zip(smooth, lap)]
     )
 
-    for kind, whole in enumerate((pack_r, halo_r, next_r)):
-        pltpu.make_async_copy(whole, whole, send_sem.at[kind]).wait()
+    def sent(kind, *wholes):
+        for whole in wholes:
+            pltpu.make_async_copy(whole, whole, send_sem.at[kind]).wait()
+
+    sent(0, pack_r)
+    sent(1, halo_r.at[pl.ds(0, 2)])
+    sent(2, next_r)
+
+    @pl.when(jnp.logical_not(is_last))
+    def _():
+        sent(1, halo_r.at[2])
+
+    @pl.when(is_last)
+    def _():
+        sent(3, list_v, field_v, slot_v, weight_v, part_s)
+
+    @pl.when(is_before)
+    def _():
+        sent(3, halo_s.at[1])
 
 
 def shards(n_wide, positions, volumes, phase_field, stencil_weights, stencil_slots, send_lists):
@@ -303,11 +415,23 @@
             pltpu.VMEM((3, 2, 4, LANES), f32),
             pltpu.VMEM((1, own), f32),
             pltpu.VMEM((n_peers, 1, own), f32),
+            pltpu.VMEM(stencil_weights.shape, f32),
+            pltpu.VMEM(stencil_slots.shape, jnp.int32),
+            pltpu.VMEM((2, own), jnp.int32),
+            pltpu.VMEM((1, own), f32),
+            pltpu.VMEM((1, own), f32),
+            pltpu.VMEM((4, LANES), f32),
+            pltpu.VMEM((3, 2, *stencil_weights.shape), f32),
+            pltpu.VMEM(stencil_slots.shape, jnp.int32),
+            pltpu.VMEM((8, LANES), jnp.int32),
+            pltpu.VMEM((1, own), f32),
+            pltpu.VMEM((1, own), f32),
             pltpu.SemaphoreType.DMA((6,)),
-            pltpu.SemaphoreType.DMA((3,)),
+            pltpu.SemaphoreType.DMA((4,)),
             pltpu.SemaphoreType.DMA((n_peers,)),
             pltpu.SemaphoreType.DMA((3, 2)),
             pltpu.SemaphoreType.DMA((n_peers,)),
+            pltpu.SemaphoreType.DMA((6,)),
         ],
         compiler_params=pltpu.CompilerParams(
             collective_id=0, has_side_effects=True, vmem_limit_bytes=16 * 1024 * 1024

time: 28.8 us -> 26.2 us (0.910)
  Pallas kernels: 27.4 us -> 24.9 us
    pallas_call x1, Pallas kernels: 27.4 us -> 24.9 us  [shards(): pl.pallas_call(functools.partial(step_kernel, n_wide, kernel_decay), out_...]
where the time goes in v4:
time: 26.2 us; the launch traced here: 26.1 us
  Pallas kernels  24.9 us (95%)
  between operations  0.64 us (2%)
  local copies, waits for them, and re-layouts  0.57 us (2%)
    pallas_call x1, Pallas kernels, shards(): pl.pallas_call(functools.partial(step_kernel, n_wide, kernel_decay), out_...  24.9 us
    slice x1, local copies, waits for them, and re-layouts, shards(): return (both[:own], both[own:])  0.57 us

profile of v4, /device:TPU:8, one launch (start us, length us, event | category | flops | bytes accessed | tf_op | source)
XLA Modules:
  0.0 26.1 jit_solution(17188116308434033695)
XLA Ops:
  0.6 24.9 %shard_map.77 = f32[2,1,256]{2,1,0:T(1,128)S(1)} custom-call(f32[3,256]{1,0:T(4,128)} %pos_h.1, f32[1,256]{1,0:T(1,128)} %bitcast.4, f32[1,256]{1,0:T(1,128)} %bitcast.5, f32[64,256]{1,0:T(8,128)} %weight_h.1, s32[64,256]{1,0:T(8,128)} %slot_h.1, s32[2,256]{1,0:T(2,128)} %list_h.1), custom_call_target="tpu_custom_call" | custom-call | tf_op jit(solution)/shard_map/pallas_call | solution.py:394
  25.5 0.6 %fusion = (f32[1,1,256]{2,1,0:T(1,128)}, f32[1,1,256]{2,1,0:T(1,128)}) fusion(f32[2,1,256]{2,1,0:T(1,128)S(1)} %shard_map.77), kind=kLoop, calls=%fused_computation | loop fusion | bytes 4096 | tf_op jit(solution)/shard_map/slice | solution.py:453

commit v5 on v4

--- a/solution.py
+++ b/solution.py
@@ -38,9 +38,9 @@
     pos_v, vol_v, field_v, weight_v, slot_v, list_v,
     pack_s, pack_r, column, gauss, acc, masked, lane_of, pick,
     halo_s, halo_r, next_s, next_r,
-    edge_weight, edge_slot, edge_list, edge_field, edge_part, edge_halo,
-    edge_masked, edge_lane, edge_pick, edge_now, part_s,
-    load_sem, send_sem, pack_rs, halo_rs, next_rs, edge_rs,
+    edge_weight, edge_slot, edge_list, edge_pack, edge_halo, edge_packs,
+    edge_masked, edge_lane, edge_pick, edge_now,
+    load_sem, send_sem, pack_rs, halo_rs, next_rs, edge_rs, edge_packs_rs, go_sem,
 ):
     wide = lax.axis_index("wide")
     narrow = lax.axis_index("narrow")
@@ -56,8 +56,14 @@
     first = (0, narrow)
 
     barrier = pltpu.get_barrier_semaphore()
-    for target in (up, down, *reversed(peers)):
-        pl.semaphore_signal(barrier, inc=1, device_id=target, device_id_type=MESH)
+    greeted = wide - jnp.where(is_last, 1, 0)
+    for _, at in reversed(peers):
+        pl.semaphore_signal(barrier, inc=1, device_id=(greeted, at), device_id_type=MESH)
+    pl.semaphore_signal(barrier, inc=1, device_id=down, device_id_type=MESH)
+
+    @pl.when(jnp.logical_not(is_last))
+    def _():
+        pl.semaphore_signal(barrier, inc=1, device_id=up, device_id_type=MESH)
 
     loads = [
         pltpu.make_async_copy(src, dst, load_sem.at[i])
@@ -92,14 +98,19 @@
         halo_s[turn] = listed(rows, pick[...])[:4]
 
     def start_halo(turn):
-        copies = halo_copies(turn)
-        copies[1].start()
+        up_copy, down_copy = halo_copies(turn)
         if turn == 0:
-            copies[0].start()
+            up_copy.start()
+
+            @pl.when(jnp.logical_not(is_first))
+            def _():
+                down_copy.start()
         else:
+            down_copy.start()
+
             @pl.when(jnp.logical_not(is_last))
             def _():
-                copies[0].start()
+                up_copy.start()
 
     def edge_copy(i, src, dst):
         return pltpu.make_async_remote_copy(
@@ -115,8 +126,9 @@
         edge_copy(i, src, dst)
         for i, (src, dst) in enumerate(
             (
-                (list_v, edge_list), (field_v, edge_field), (slot_v, edge_slot),
-                (weight_v, edge_weight), (part_s, edge_part), (halo_s.at[1], edge_halo),
+                (pack_s, edge_pack), (list_v, edge_list), (slot_v, edge_slot),
+                (weight_v, edge_weight), (halo_s.at[0], edge_halo.at[0]),
+                (halo_s.at[1], edge_halo.at[1]),
             )
         )
     ]
@@ -166,7 +178,17 @@
     def add(*lists):
         return [functools.reduce(jnp.add, parts) for parts in zip(*lists)]
 
-    def add_sources(slot, source):
+    def edge_lap(turn, rows):
+        pairs = (
+            halves(rows),
+            [edge_halo[turn, h:h + 1] for h in range(2)],
+            [halo_s[turn, 2 + h:3 + h] for h in range(2)],
+        )
+        return add(*(
+            lap_part(pair, kind, rows, edge_lane, edge_masked) for kind, pair in enumerate(pairs)
+        ))
+
+    def add_sources(slot, source, keep=True):
         rows = [halves(source[r]) for r in range(5)]
         for t in range(0, 256, CHUNK):
             span = slice(t, t + CHUNK)
@@ -177,7 +199,8 @@
                 distance = distance + (column[1, span] - sy) ** 2
                 distance = distance + (column[2, span] - sz) ** 2
                 value = jnp.exp2(distance * (-kernel_decay * LOG2_E)) * sv
-                gauss[slot, at, span] = value
+                if keep:
+                    gauss[slot, at, span] = value
                 term = value * (column[3, span] - sf)
                 total = term if total is None else total + term
             if slot == 7:
@@ -216,7 +239,15 @@
     pack_s[3] = vol_v[...]
     pack_s[4] = field
 
-    pl.semaphore_wait(barrier, 2 + len(peers))
+    n_peers = len(peers)
+    greetings = jnp.where(
+        is_last, 2, jnp.where(is_before, 2 + 2 * n_peers, jnp.where(is_first, 1, 2) + n_peers)
+    )
+    pl.semaphore_wait(barrier, greetings)
+
+    @pl.when(is_before)
+    def _():
+        pl.semaphore_signal(go_sem, inc=1, device_id=up, device_id_type=MESH)
 
     pack_copies = [
         pltpu.make_async_remote_copy(
@@ -240,27 +271,65 @@
         )
         for i, target in enumerate(peers)
     ]
+    edge_pack_copies = [
+        pltpu.make_async_remote_copy(
+            src_ref=edge_pack,
+            dst_ref=edge_packs.at[i],
+            send_sem=send_sem.at[3],
+            recv_sem=edge_packs_rs.at[i],
+            device_id=target,
+            device_id_type=MESH,
+        )
+        for i, target in enumerate(peers)
+    ]
+
+    @pl.when(is_last)
+    def _():
+        edge_copies[0].start()
+
+    @pl.when(is_last)
+    def _():
+        start_halo(0)
+        edge_copies[1].start()
+        loads[4].wait()
+        edge_copies[2].start()
+        loads[5].wait()
+        edge_copies[3].start()
+        pl.semaphore_wait(go_sem, 1)
+
     for copy in reversed(pack_copies):
         copy.start()
-    start_halo(0)
-    loads[4].wait()
-    loads[5].wait()
-
-    @pl.when(is_last)
-    def _():
-        for i in range(4):
-            edge_copies[i].start()
-
-    for r, row in enumerate((pos_v[0:1], pos_v[1:2], pos_v[2:3], field)):
-        for at, part in enumerate(halves(row)):
-            column[r, at * LANES:(at + 1) * LANES] = jnp.broadcast_to(part, (LANES, LANES)).T
+
+    @pl.when(jnp.logical_not(is_last))
+    def _():
+        start_halo(0)
+
+        @pl.when(is_before)
+        def _():
+            halo_wait(0, 1)
+            edge_copies[4].start()
+
+        loads[4].wait()
+        loads[5].wait()
+
+    def set_column(source):
+        for r, row in enumerate((source[0], source[1], source[2], source[4])):
+            for at, part in enumerate(halves(row)):
+                span = slice(at * LANES, (at + 1) * LANES)
+                column[r, span] = jnp.broadcast_to(part, (LANES, LANES)).T
+
+    set_column(pack_s)
     add_sources(7, pack_s)
     set_stencil(masked, lane_of, slot_v[...], weight_v[...])
     lap = lap_part(halves(field), 0, field)
     for i in range(5):
         pack_copies[i].wait_recv()
         add_sources(i, pack_r.at[i])
-    halo_wait(0, near_side)
+
+    @pl.when(jnp.logical_not(is_before))
+    def _():
+        halo_wait(0, near_side)
+
     lap = add(lap, lap_side(0, near_side, field))
     for i in range(5, 7):
         pack_copies[i].wait_recv()
@@ -269,12 +338,19 @@
         [kernel_strength * a - gradient_energy * b for a, b in zip(fold(acc[...]), lap)]
     )
 
-    @pl.when(is_last)
-    def _():
-        part_s[...] = part
-        edge_copies[4].start()
+    @pl.when(is_first)
+    def _():
+        edge_copies[0].wait_recv()
+        for copy in reversed(edge_pack_copies):
+            copy.start()
 
     halo_wait(0, far_side)
+
+    @pl.when(is_first)
+    def _():
+        _, down_copy = halo_copies(0)
+        down_copy.start()
+
     now = part - gradient_energy * finish(lap_side(0, far_side, field))
 
     to_halo(now, 1)
@@ -301,15 +377,26 @@
 
     @pl.when(is_first)
     def _():
-        for i in range(4):
+        set_column(edge_pack)
+        add_sources(7, edge_pack, keep=False)
+        for i in range(3):
+            edge_pack_copies[i].wait_recv()
+            add_sources(i, edge_packs.at[i], keep=False)
+        for i in range(1, 5):
             edge_copies[i].wait_recv()
         set_pick(edge_pick, edge_list[...])
         set_stencil(edge_masked, edge_lane, edge_slot[...], edge_weight[...])
-        theirs = edge_field[...]
-        rows = [halo_s[0, 2 + h:3 + h] for h in range(2)]
-        high = finish(lap_part(rows, 2, theirs, edge_lane, edge_masked))
-        edge_copies[4].wait_recv()
-        theirs_now = edge_part[...] - gradient_energy * high
+        theirs = edge_pack[4]
+        their_lap = edge_lap(0, theirs)
+        for i in range(3, n_peers):
+            edge_pack_copies[i].wait_recv()
+            add_sources(i, edge_packs.at[i], keep=False)
+        theirs_now = theirs * theirs * theirs - theirs + finish(
+            [
+                kernel_strength * a - gradient_energy * b
+                for a, b in zip(fold(acc[...]), their_lap)
+            ]
+        )
         edge_now[...] = theirs_now
         halo_r[1, 0] = listed(theirs_now, edge_pick[...])[:4]
 
@@ -329,16 +416,7 @@
     def _():
         theirs_now = edge_now[...]
         edge_copies[5].wait_recv()
-        rows = [
-            halves(theirs_now),
-            [edge_halo[h:h + 1] for h in range(2)],
-            [halo_s[1, 2 + h:3 + h] for h in range(2)],
-        ]
-        lap_next = add(*(
-            lap_part(pair, kind, theirs_now, edge_lane, edge_masked)
-            for kind, pair in enumerate(rows)
-        ))
-        theirs_after = edge_field[...] + time_step * finish(lap_next)
+        theirs_after = edge_pack[4] + time_step * finish(edge_lap(1, theirs_now))
         halo_r[2, 0] = listed(theirs_after, edge_pick[...])[:4]
 
     for i in range(3):
@@ -376,11 +454,15 @@
 
     @pl.when(is_last)
     def _():
-        sent(3, list_v, field_v, slot_v, weight_v, part_s)
+        sent(3, pack_s, list_v, slot_v, weight_v)
 
     @pl.when(is_before)
     def _():
-        sent(3, halo_s.at[1])
+        sent(3, halo_s.at[pl.ds(0, 2)])
+
+    @pl.when(is_first)
+    def _():
+        sent(3, edge_packs)
 
 
 def shards(n_wide, positions, volumes, phase_field, stencil_weights, stencil_slots, send_lists):
@@ -418,13 +500,12 @@
             pltpu.VMEM(stencil_weights.shape, f32),
             pltpu.VMEM(stencil_slots.shape, jnp.int32),
             pltpu.VMEM((2, own), jnp.int32),
-            pltpu.VMEM((1, own), f32),
-            pltpu.VMEM((1, own), f32),
-            pltpu.VMEM((4, LANES), f32),
+            pltpu.VMEM((5, 1, own), f32),
+            pltpu.VMEM((2, 4, LANES), f32),
+            pltpu.VMEM((n_peers, 5, 1, own), f32),
             pltpu.VMEM((3, 2, *stencil_weights.shape), f32),
             pltpu.VMEM(stencil_slots.shape, jnp.int32),
             pltpu.VMEM((8, LANES), jnp.int32),
-            pltpu.VMEM((1, own), f32),
             pltpu.VMEM((1, own), f32),
             pltpu.SemaphoreType.DMA((6,)),
             pltpu.SemaphoreType.DMA((4,)),
@@ -432,6 +513,8 @@
             pltpu.SemaphoreType.DMA((3, 2)),
             pltpu.SemaphoreType.DMA((n_peers,)),
             pltpu.SemaphoreType.DMA((6,)),
+            pltpu.SemaphoreType.DMA((n_peers,)),
+            pltpu.SemaphoreType.REGULAR,
         ],
         compiler_params=pltpu.CompilerParams(
             collective_id=0, has_side_effects=True, vmem_limit_bytes=16 * 1024 * 1024

time: 26.2 us -> 25.7 us (0.981)
  Pallas kernels: 24.9 us -> 24.3 us
    pallas_call x1, Pallas kernels: 24.9 us -> 24.3 us  [shards(): pl.pallas_call(functools.partial(step_kernel, n_wide, kernel_decay), out_...]
where the time goes in v5:
time: 25.7 us; the launch traced here: 25.5 us
  Pallas kernels  24.3 us (95%)
  between operations  0.64 us (2%)
  local copies, waits for them, and re-layouts  0.57 us (2%)
    pallas_call x1, Pallas kernels, shards(): pl.pallas_call(functools.partial(step_kernel, n_wide, kernel_decay), out_...  24.3 us
    slice x1, local copies, waits for them, and re-layouts, shards(): return (both[:own], both[own:])  0.57 us

profile of v5, /device:TPU:8, one launch (start us, length us, event | category | flops | bytes accessed | tf_op | source)
XLA Modules:
  0.0 25.5 jit_solution(14192120371701884210)
XLA Ops:
  0.6 24.3 %shard_map.77 = f32[2,1,256]{2,1,0:T(1,128)S(1)} custom-call(f32[3,256]{1,0:T(4,128)} %pos_h.1, f32[1,256]{1,0:T(1,128)} %bitcast.4, f32[1,256]{1,0:T(1,128)} %bitcast.5, f32[64,256]{1,0:T(8,128)} %weight_h.1, s32[64,256]{1,0:T(8,128)} %slot_h.1, s32[2,256]{1,0:T(2,128)} %list_h.1), custom_call_target="tpu_custom_call" | custom-call | tf_op jit(solution)/shard_map/pallas_call | solution.py:476
  24.9 0.6 %fusion = (f32[1,1,256]{2,1,0:T(1,128)}, f32[1,1,256]{2,1,0:T(1,128)}) fusion(f32[2,1,256]{2,1,0:T(1,128)S(1)} %shard_map.77), kind=kLoop, calls=%fused_computation | loop fusion | bytes 4096 | tf_op jit(solution)/shard_map/slice | solution.py:536

commit v6 on v5

--- a/solution.py
+++ b/solution.py
@@ -38,7 +38,7 @@
     pos_v, vol_v, field_v, weight_v, slot_v, list_v,
     pack_s, pack_r, column, gauss, acc, masked, lane_of, pick,
     halo_s, halo_r, next_s, next_r,
-    edge_weight, edge_slot, edge_list, edge_pack, edge_halo, edge_packs,
+    edge_weight, edge_slot, edge_list, edge_pos, edge_vol, edge_field, edge_pack, edge_halo, edge_packs,
     edge_masked, edge_lane, edge_pick, edge_now,
     load_sem, send_sem, pack_rs, halo_rs, next_rs, edge_rs, edge_packs_rs, go_sem,
 ):
@@ -54,16 +54,7 @@
     far_side = 1 - near_side
     is_first, is_last, is_before = wide == 0, wide == n_wide - 1, wide == n_wide - 2
     first = (0, narrow)
-
-    barrier = pltpu.get_barrier_semaphore()
-    greeted = wide - jnp.where(is_last, 1, 0)
-    for _, at in reversed(peers):
-        pl.semaphore_signal(barrier, inc=1, device_id=(greeted, at), device_id_type=MESH)
-    pl.semaphore_signal(barrier, inc=1, device_id=down, device_id_type=MESH)
-
-    @pl.when(jnp.logical_not(is_last))
-    def _():
-        pl.semaphore_signal(barrier, inc=1, device_id=up, device_id_type=MESH)
+    before = (n_wide - 2, narrow)
 
     loads = [
         pltpu.make_async_copy(src, dst, load_sem.at[i])
@@ -77,10 +68,30 @@
     for load in loads:
         load.start()
 
+    barrier = pltpu.get_barrier_semaphore()
+    greeted = wide - jnp.where(is_last, 1, 0)
+    for _, at in reversed(peers):
+        pl.semaphore_signal(barrier, inc=1, device_id=(greeted, at), device_id_type=MESH)
+    pl.semaphore_signal(barrier, inc=1, device_id=down, device_id_type=MESH)
+
+    @pl.when(wide < n_wide - 2)
+    def _():
+        pl.semaphore_signal(barrier, inc=1, device_id=up, device_id_type=MESH)
+
+    @pl.when(is_first)
+    def _():
+        pl.semaphore_signal(barrier, inc=1, device_id=before, device_id_type=MESH)
+
     def listed(rows, pairs):
         low, high = halves(rows)
         lanes = pairs & (LANES - 1)
         return jnp.where(pairs >= LANES, lookup(high, lanes), lookup(low, lanes))
+
+    def set_pack(into, pos, vol, rows):
+        for r in range(3):
+            into[r] = pos[r:r + 1]
+        into[3] = vol
+        into[4] = rows
 
     def set_pick(into, lists):
         for r in range(2):
@@ -102,7 +113,7 @@
         if turn == 0:
             up_copy.start()
 
-            @pl.when(jnp.logical_not(is_first))
+            @pl.when(jnp.logical_not(is_first | is_last))
             def _():
                 down_copy.start()
         else:
@@ -126,9 +137,9 @@
         edge_copy(i, src, dst)
         for i, (src, dst) in enumerate(
             (
-                (pack_s, edge_pack), (list_v, edge_list), (slot_v, edge_slot),
-                (weight_v, edge_weight), (halo_s.at[0], edge_halo.at[0]),
-                (halo_s.at[1], edge_halo.at[1]),
+                (pos_h, edge_pos), (vol_h, edge_vol), (field_h, edge_field), (list_h, edge_list),
+                (slot_h, edge_slot), (weight_h, edge_weight),
+                (halo_s.at[0], edge_halo.at[0]), (halo_s.at[1], edge_halo.at[1]),
             )
         )
     ]
@@ -178,15 +189,14 @@
     def add(*lists):
         return [functools.reduce(jnp.add, parts) for parts in zip(*lists)]
 
-    def edge_lap(turn, rows):
-        pairs = (
-            halves(rows),
-            [edge_halo[turn, h:h + 1] for h in range(2)],
-            [halo_s[turn, 2 + h:3 + h] for h in range(2)],
-        )
-        return add(*(
-            lap_part(pair, kind, rows, edge_lane, edge_masked) for kind, pair in enumerate(pairs)
-        ))
+    def edge_lap(turn, rows, kind):
+        if kind == 0:
+            pair = halves(rows)
+        elif kind == 1:
+            pair = [edge_halo[turn, h:h + 1] for h in range(2)]
+        else:
+            pair = [halo_s[turn, 2 + h:3 + h] for h in range(2)]
+        return lap_part(pair, kind, rows, edge_lane, edge_masked)
 
     def add_sources(slot, source, keep=True):
         rows = [halves(source[r]) for r in range(5)]
@@ -227,6 +237,12 @@
     def finish(parts):
         return join([jnp.sum(part, axis=0, keepdims=True) for part in parts])
 
+    @pl.when(is_last)
+    def _():
+        pl.semaphore_wait(barrier, 1)
+        for i in range(3):
+            edge_copies[i].start()
+
     loads[0].wait()
     loads[1].wait()
     set_pick(pick, list_v[...])
@@ -234,20 +250,19 @@
     to_halo(field, 0)
     loads[2].wait()
     loads[3].wait()
-    for r in range(3):
-        pack_s[r] = pos_v[r:r + 1]
-    pack_s[3] = vol_v[...]
-    pack_s[4] = field
+    set_pack(pack_s, pos_v, vol_v[...], field)
 
     n_peers = len(peers)
-    greetings = jnp.where(
-        is_last, 2, jnp.where(is_before, 2 + 2 * n_peers, jnp.where(is_first, 1, 2) + n_peers)
-    )
-    pl.semaphore_wait(barrier, greetings)
+    greetings = jnp.where(is_before, 3 + 2 * n_peers, jnp.where(is_first, 1, 2) + n_peers)
+
+    @pl.when(jnp.logical_not(is_last))
+    def _():
+        pl.semaphore_wait(barrier, greetings)
 
     @pl.when(is_before)
     def _():
         pl.semaphore_signal(go_sem, inc=1, device_id=up, device_id_type=MESH)
+        edge_copies[6].start()
 
     pack_copies = [
         pltpu.make_async_remote_copy(
@@ -285,17 +300,13 @@
 
     @pl.when(is_last)
     def _():
-        edge_copies[0].start()
-
-    @pl.when(is_last)
-    def _():
         start_halo(0)
-        edge_copies[1].start()
+        for i in range(3, 6):
+            edge_copies[i].start()
         loads[4].wait()
-        edge_copies[2].start()
         loads[5].wait()
-        edge_copies[3].start()
         pl.semaphore_wait(go_sem, 1)
+        halo_copies(0)[1].start()
 
     for copy in reversed(pack_copies):
         copy.start()
@@ -303,11 +314,6 @@
     @pl.when(jnp.logical_not(is_last))
     def _():
         start_halo(0)
-
-        @pl.when(is_before)
-        def _():
-            halo_wait(0, 1)
-            edge_copies[4].start()
 
         loads[4].wait()
         loads[5].wait()
@@ -325,11 +331,7 @@
     for i in range(5):
         pack_copies[i].wait_recv()
         add_sources(i, pack_r.at[i])
-
-    @pl.when(jnp.logical_not(is_before))
-    def _():
-        halo_wait(0, near_side)
-
+    halo_wait(0, near_side)
     lap = add(lap, lap_side(0, near_side, field))
     for i in range(5, 7):
         pack_copies[i].wait_recv()
@@ -340,7 +342,9 @@
 
     @pl.when(is_first)
     def _():
-        edge_copies[0].wait_recv()
+        for i in range(3):
+            edge_copies[i].wait_recv()
+        set_pack(edge_pack, edge_pos, edge_vol[...], edge_field[...])
         for copy in reversed(edge_pack_copies):
             copy.start()
 
@@ -358,7 +362,7 @@
 
     @pl.when(is_before)
     def _():
-        edge_copies[5].start()
+        edge_copies[7].start()
 
     lap = lap_part(halves(now), 0, now)
     halo_wait(1, near_side)
@@ -382,15 +386,19 @@
         for i in range(3):
             edge_pack_copies[i].wait_recv()
             add_sources(i, edge_packs.at[i], keep=False)
-        for i in range(1, 5):
+        for i in range(3, 6):
             edge_copies[i].wait_recv()
         set_pick(edge_pick, edge_list[...])
         set_stencil(edge_masked, edge_lane, edge_slot[...], edge_weight[...])
         theirs = edge_pack[4]
-        their_lap = edge_lap(0, theirs)
-        for i in range(3, n_peers):
+        their_lap = add(edge_lap(0, theirs, 0), edge_lap(0, theirs, 2))
+        for i in range(3, 6):
             edge_pack_copies[i].wait_recv()
             add_sources(i, edge_packs.at[i], keep=False)
+        edge_copies[6].wait_recv()
+        their_lap = add(their_lap, edge_lap(0, theirs, 1))
+        edge_pack_copies[6].wait_recv()
+        add_sources(6, edge_packs.at[6], keep=False)
         theirs_now = theirs * theirs * theirs - theirs + finish(
             [
                 kernel_strength * a - gradient_energy * b
@@ -415,8 +423,10 @@
     @pl.when(is_first)
     def _():
         theirs_now = edge_now[...]
-        edge_copies[5].wait_recv()
-        theirs_after = edge_pack[4] + time_step * finish(edge_lap(1, theirs_now))
+        their_lap = add(edge_lap(1, theirs_now, 0), edge_lap(1, theirs_now, 2))
+        edge_copies[7].wait_recv()
+        their_lap = add(their_lap, edge_lap(1, theirs_now, 1))
+        theirs_after = edge_pack[4] + time_step * finish(their_lap)
         halo_r[2, 0] = listed(theirs_after, edge_pick[...])[:4]
 
     for i in range(3):
@@ -454,7 +464,7 @@
 
     @pl.when(is_last)
     def _():
-        sent(3, pack_s, list_v, slot_v, weight_v)
+        sent(3, pos_v, vol_v, field_v, list_v, slot_v, weight_v)
 
     @pl.when(is_before)
     def _():
@@ -500,6 +510,9 @@
             pltpu.VMEM(stencil_weights.shape, f32),
             pltpu.VMEM(stencil_slots.shape, jnp.int32),
             pltpu.VMEM((2, own), jnp.int32),
+            pltpu.VMEM((3, own), f32),
+            pltpu.VMEM((1, own), f32),
+            pltpu.VMEM((1, own), f32),
             pltpu.VMEM((5, 1, own), f32),
             pltpu.VMEM((2, 4, LANES), f32),
             pltpu.VMEM((n_peers, 5, 1, own), f32),
@@ -512,7 +525,7 @@
             pltpu.SemaphoreType.DMA((n_peers,)),
             pltpu.SemaphoreType.DMA((3, 2)),
             pltpu.SemaphoreType.DMA((n_peers,)),
-            pltpu.SemaphoreType.DMA((6,)),
+            pltpu.SemaphoreType.DMA((8,)),
             pltpu.SemaphoreType.DMA((n_peers,)),
             pltpu.SemaphoreType.REGULAR,
         ],

time: 25.7 us -> 25.2 us (0.981)
  Pallas kernels: 24.3 us -> 23.9 us
    pallas_call x1, Pallas kernels: 24.3 us -> 23.9 us  [shards(): pl.pallas_call(functools.partial(step_kernel, n_wide, kernel_decay), out_...]
where the time goes in v6:
time: 25.2 us; the launch traced here: 25.1 us
  Pallas kernels  23.9 us (95%)
  between operations  0.64 us (3%)
  local copies, waits for them, and re-layouts  0.57 us (2%)
    pallas_call x1, Pallas kernels, shards(): pl.pallas_call(functools.partial(step_kernel, n_wide, kernel_decay), out_...  23.9 us
    slice x1, local copies, waits for them, and re-layouts, shards(): return (both[:own], both[own:])  0.57 us

profile of v6, /device:TPU:8, one launch (start us, length us, event | category | flops | bytes accessed | tf_op | source)
XLA Modules:
  0.0 25.1 jit_solution(15881201808859932934)
XLA Ops:
  0.6 23.9 %shard_map.77 = f32[2,1,256]{2,1,0:T(1,128)S(1)} custom-call(f32[3,256]{1,0:T(4,128)} %pos_h.1, f32[1,256]{1,0:T(1,128)} %bitcast.4, f32[1,256]{1,0:T(1,128)} %bitcast.5, f32[64,256]{1,0:T(8,128)} %weight_h.1, s32[64,256]{1,0:T(8,128)} %slot_h.1, s32[2,256]{1,0:T(2,128)} %list_h.1), custom_call_target="tpu_custom_call" | custom-call | tf_op jit(solution)/shard_map/pallas_call | solution.py:486
  24.5 0.6 %fusion = (f32[1,1,256]{2,1,0:T(1,128)}, f32[1,1,256]{2,1,0:T(1,128)}) fusion(f32[2,1,256]{2,1,0:T(1,128)S(1)} %shard_map.77), kind=kLoop, calls=%fused_computation | loop fusion | bytes 4096 | tf_op jit(solution)/shard_map/slice | solution.py:549

commit v7 on v6

--- a/solution.py
+++ b/solution.py
@@ -13,7 +13,8 @@
 LANES = 128
 MESH = pl.DeviceIdType.MESH
 PEERS = ((0, 1), (1, 0), (3, 0), (1, 1), (3, 1), (2, 0), (2, 1))
-CHUNK = 64
+CHUNK = 128
+GROUPS = (range(0, 3), range(3, 6), range(6, 7))
 LOG2_E = 1.4426950408889634
 
 
@@ -29,6 +30,10 @@
 
 def join(pair):
     return jnp.concatenate(pair, axis=1)
+
+
+def await_bytes(ref, sem):
+    pltpu.make_async_copy(ref, ref, sem).wait()
 
 
 def step_kernel(
@@ -57,12 +62,10 @@
     before = (n_wide - 2, narrow)
 
     loads = [
-        pltpu.make_async_copy(src, dst, load_sem.at[i])
-        for i, (src, dst) in enumerate(
-            (
-                (list_h, list_v), (field_h, field_v), (pos_h, pos_v), (vol_h, vol_v),
-                (slot_h, slot_v), (weight_h, weight_v),
-            )
+        pltpu.make_async_copy(src, dst, load_sem.at[kind])
+        for kind, src, dst in (
+            (0, list_h, list_v), (0, field_h, field_v), (0, vol_h, vol_v), (1, pos_h, pos_v),
+            (2, slot_h, slot_v), (2, weight_h, weight_v),
         )
     ]
     for load in loads:
@@ -127,20 +130,18 @@
         return pltpu.make_async_remote_copy(
             src_ref=src,
             dst_ref=dst,
-            send_sem=send_sem.at[3],
+            send_sem=send_sem,
             recv_sem=edge_rs.at[i],
             device_id=first,
             device_id_type=MESH,
         )
 
     edge_copies = [
-        edge_copy(i, src, dst)
-        for i, (src, dst) in enumerate(
-            (
-                (pos_h, edge_pos), (vol_h, edge_vol), (field_h, edge_field), (list_h, edge_list),
-                (slot_h, edge_slot), (weight_h, edge_weight),
-                (halo_s.at[0], edge_halo.at[0]), (halo_s.at[1], edge_halo.at[1]),
-            )
+        edge_copy(kind, src, dst)
+        for kind, src, dst in (
+            (0, pos_h, edge_pos), (1, vol_h, edge_vol), (1, field_h, edge_field),
+            (1, list_h, edge_list), (2, slot_h, edge_slot), (2, weight_h, edge_weight),
+            (3, halo_s.at[0], edge_halo.at[0]), (4, halo_s.at[1], edge_halo.at[1]),
         )
     ]
 
@@ -149,7 +150,7 @@
             pltpu.make_async_remote_copy(
                 src_ref=halo_s.at[turn],
                 dst_ref=halo_r.at[turn, side],
-                send_sem=send_sem.at[1],
+                send_sem=send_sem,
                 recv_sem=halo_rs.at[turn, side],
                 device_id=target,
                 device_id_type=MESH,
@@ -161,7 +162,7 @@
         pltpu.make_async_remote_copy(
             src_ref=halo_s.at[turn],
             dst_ref=halo_r.at[turn, side],
-            send_sem=send_sem.at[1],
+            send_sem=send_sem,
             recv_sem=halo_rs.at[turn, side],
             device_id=up,
             device_id_type=MESH,
@@ -240,15 +241,13 @@
     @pl.when(is_last)
     def _():
         pl.semaphore_wait(barrier, 1)
-        for i in range(3):
-            edge_copies[i].start()
-
-    loads[0].wait()
-    loads[1].wait()
+        for copy in edge_copies[:4]:
+            copy.start()
+
+    await_bytes(pack_s.at[pl.ds(0, 4)], load_sem.at[0])
     set_pick(pick, list_v[...])
     field = field_v[...]
     to_halo(field, 0)
-    loads[2].wait()
     loads[3].wait()
     set_pack(pack_s, pos_v, vol_v[...], field)
 
@@ -268,8 +267,8 @@
         pltpu.make_async_remote_copy(
             src_ref=pack_s,
             dst_ref=pack_r.at[i],
-            send_sem=send_sem.at[0],
-            recv_sem=pack_rs.at[i],
+            send_sem=send_sem,
+            recv_sem=pack_rs.at[i // 3],
             device_id=target,
             device_id_type=MESH,
         )
@@ -279,8 +278,8 @@
         pltpu.make_async_remote_copy(
             src_ref=next_s,
             dst_ref=next_r.at[i],
-            send_sem=send_sem.at[2],
-            recv_sem=next_rs.at[i],
+            send_sem=send_sem,
+            recv_sem=next_rs.at[i // 3],
             device_id=target,
             device_id_type=MESH,
         )
@@ -290,8 +289,8 @@
         pltpu.make_async_remote_copy(
             src_ref=edge_pack,
             dst_ref=edge_packs.at[i],
-            send_sem=send_sem.at[3],
-            recv_sem=edge_packs_rs.at[i],
+            send_sem=send_sem,
+            recv_sem=edge_packs_rs.at[i // 3],
             device_id=target,
             device_id_type=MESH,
         )
@@ -301,10 +300,9 @@
     @pl.when(is_last)
     def _():
         start_halo(0)
-        for i in range(3, 6):
-            edge_copies[i].start()
-        loads[4].wait()
-        loads[5].wait()
+        for copy in edge_copies[4:6]:
+            copy.start()
+        await_bytes(masked.at[0], load_sem.at[2])
         pl.semaphore_wait(go_sem, 1)
         halo_copies(0)[1].start()
 
@@ -315,8 +313,7 @@
     def _():
         start_halo(0)
 
-        loads[4].wait()
-        loads[5].wait()
+        await_bytes(masked.at[0], load_sem.at[2])
 
     def set_column(source):
         for r, row in enumerate((source[0], source[1], source[2], source[4])):
@@ -328,13 +325,17 @@
     add_sources(7, pack_s)
     set_stencil(masked, lane_of, slot_v[...], weight_v[...])
     lap = lap_part(halves(field), 0, field)
-    for i in range(5):
-        pack_copies[i].wait_recv()
-        add_sources(i, pack_r.at[i])
+    def of_group(group, buffer, sems):
+        members = GROUPS[group]
+        await_bytes(buffer.at[pl.ds(members.start, len(members))], sems.at[group])
+        return members
+
+    for group in range(2):
+        for i in of_group(group, pack_r, pack_rs):
+            add_sources(i, pack_r.at[i])
     halo_wait(0, near_side)
     lap = add(lap, lap_side(0, near_side, field))
-    for i in range(5, 7):
-        pack_copies[i].wait_recv()
+    for i in of_group(2, pack_r, pack_rs):
         add_sources(i, pack_r.at[i])
     part = field * field * field - field + finish(
         [kernel_strength * a - gradient_energy * b for a, b in zip(fold(acc[...]), lap)]
@@ -342,8 +343,8 @@
 
     @pl.when(is_first)
     def _():
-        for i in range(3):
-            edge_copies[i].wait_recv()
+        edge_copies[0].wait_recv()
+        await_bytes(pack_s.at[pl.ds(0, 4)], edge_rs.at[1])
         set_pack(edge_pack, edge_pos, edge_vol[...], edge_field[...])
         for copy in reversed(edge_pack_copies):
             copy.start()
@@ -383,22 +384,19 @@
     def _():
         set_column(edge_pack)
         add_sources(7, edge_pack, keep=False)
-        for i in range(3):
-            edge_pack_copies[i].wait_recv()
+        for i in of_group(0, edge_packs, edge_packs_rs):
             add_sources(i, edge_packs.at[i], keep=False)
-        for i in range(3, 6):
-            edge_copies[i].wait_recv()
+        await_bytes(edge_masked.at[0], edge_rs.at[2])
         set_pick(edge_pick, edge_list[...])
         set_stencil(edge_masked, edge_lane, edge_slot[...], edge_weight[...])
         theirs = edge_pack[4]
         their_lap = add(edge_lap(0, theirs, 0), edge_lap(0, theirs, 2))
-        for i in range(3, 6):
-            edge_pack_copies[i].wait_recv()
+        for i in of_group(1, edge_packs, edge_packs_rs):
             add_sources(i, edge_packs.at[i], keep=False)
         edge_copies[6].wait_recv()
         their_lap = add(their_lap, edge_lap(0, theirs, 1))
-        edge_pack_copies[6].wait_recv()
-        add_sources(6, edge_packs.at[6], keep=False)
+        for i in of_group(2, edge_packs, edge_packs_rs):
+            add_sources(i, edge_packs.at[i], keep=False)
         theirs_now = theirs * theirs * theirs - theirs + finish(
             [
                 kernel_strength * a - gradient_energy * b
@@ -429,13 +427,11 @@
         theirs_after = edge_pack[4] + time_step * finish(their_lap)
         halo_r[2, 0] = listed(theirs_after, edge_pick[...])[:4]
 
-    for i in range(3):
-        next_copies[i].wait_recv()
+    for i in of_group(0, next_r, next_rs):
         add_field(i, next_r[i])
     halo_wait(2, near_side)
     lap = add(lap, lap_side(2, near_side, after))
-    for i in range(3, 6):
-        next_copies[i].wait_recv()
+    for i in of_group(1, next_r, next_rs):
         add_field(i, next_r[i])
 
     @pl.when(jnp.logical_not(is_first))
@@ -443,36 +439,34 @@
         halo_wait(2, far_side)
 
     lap = add(lap, lap_side(2, far_side, after))
-    next_copies[6].wait_recv()
-    add_field(6, next_r[6])
+    for i in of_group(2, next_r, next_rs):
+        add_field(i, next_r[i])
     smooth = fold(acc[...])
     out_o[1] = rest - finish(
         [kernel_strength * a + gradient_energy * b for a, b in zip(smooth, lap)]
     )
 
-    def sent(kind, *wholes):
+    def sent(*wholes):
         for whole in wholes:
-            pltpu.make_async_copy(whole, whole, send_sem.at[kind]).wait()
-
-    sent(0, pack_r)
-    sent(1, halo_r.at[pl.ds(0, 2)])
-    sent(2, next_r)
+            await_bytes(whole, send_sem)
+
+    sent(pack_r, halo_r.at[pl.ds(0, 2)], next_r)
 
     @pl.when(jnp.logical_not(is_last))
     def _():
-        sent(1, halo_r.at[2])
+        sent(halo_r.at[2])
 
     @pl.when(is_last)
     def _():
-        sent(3, pos_v, vol_v, field_v, list_v, slot_v, weight_v)
+        sent(pos_v, vol_v, field_v, list_v, slot_v, weight_v)
 
     @pl.when(is_before)
     def _():
-        sent(3, halo_s.at[pl.ds(0, 2)])
+        sent(halo_s.at[pl.ds(0, 2)])
 
     @pl.when(is_first)
     def _():
-        sent(3, edge_packs)
+        sent(edge_packs)
 
 
 def shards(n_wide, positions, volumes, phase_field, stencil_weights, stencil_slots, send_lists):
@@ -520,13 +514,13 @@
             pltpu.VMEM(stencil_slots.shape, jnp.int32),
             pltpu.VMEM((8, LANES), jnp.int32),
             pltpu.VMEM((1, own), f32),
-            pltpu.SemaphoreType.DMA((6,)),
-            pltpu.SemaphoreType.DMA((4,)),
-            pltpu.SemaphoreType.DMA((n_peers,)),
+            pltpu.SemaphoreType.DMA((3,)),
+            pltpu.SemaphoreType.DMA,
+            pltpu.SemaphoreType.DMA((len(GROUPS),)),
             pltpu.SemaphoreType.DMA((3, 2)),
-            pltpu.SemaphoreType.DMA((n_peers,)),
-            pltpu.SemaphoreType.DMA((8,)),
-            pltpu.SemaphoreType.DMA((n_peers,)),
+            pltpu.SemaphoreType.DMA((len(GROUPS),)),
+            pltpu.SemaphoreType.DMA((5,)),
+            pltpu.SemaphoreType.DMA((len(GROUPS),)),
             pltpu.SemaphoreType.REGULAR,
         ],
         compiler_params=pltpu.CompilerParams(

time: 25.2 us -> 25.3 us (level)
  no operation moved by 1% of the time
where the time goes in v7:
time: 25.3 us; the launch traced here: 25.1 us
  Pallas kernels  23.9 us (94%)
  between operations  0.64 us (3%)
  local copies, waits for them, and re-layouts  0.57 us (2%)
    pallas_call x1, Pallas kernels, shards(): pl.pallas_call(functools.partial(step_kernel, n_wide, kernel_decay), out_...  23.9 us
    slice x1, local copies, waits for them, and re-layouts, shards(): return (both[:own], both[own:])  0.57 us

profile of v7, /device:TPU:8, one launch (start us, length us, event | category | flops | bytes accessed | tf_op | source)
XLA Modules:
  0.0 25.1 jit_solution(5870959140122089639)
XLA Ops:
  0.6 23.9 %shard_map.77 = f32[2,1,256]{2,1,0:T(1,128)S(1)} custom-call(f32[3,256]{1,0:T(4,128)} %pos_h.1, f32[1,256]{1,0:T(1,128)} %bitcast.4, f32[1,256]{1,0:T(1,128)} %bitcast.5, f32[64,256]{1,0:T(8,128)} %weight_h.1, s32[64,256]{1,0:T(8,128)} %slot_h.1, s32[2,256]{1,0:T(2,128)} %list_h.1), custom_call_target="tpu_custom_call" | custom-call | tf_op jit(solution)/shard_map/pallas_call | solution.py:480
  24.5 0.6 %fusion = (f32[1,1,256]{2,1,0:T(1,128)}, f32[1,1,256]{2,1,0:T(1,128)}) fusion(f32[2,1,256]{2,1,0:T(1,128)S(1)} %shard_map.77), kind=kLoop, calls=%fused_computation | loop fusion | bytes 4096 | tf_op jit(solution)/shard_map/slice | solution.py:543

commit v8 on v7

--- a/solution.py
+++ b/solution.py
@@ -268,7 +268,7 @@
             src_ref=pack_s,
             dst_ref=pack_r.at[i],
             send_sem=send_sem,
-            recv_sem=pack_rs.at[i // 3],
+            recv_sem=pack_rs.at[i],
             device_id=target,
             device_id_type=MESH,
         )
@@ -290,7 +290,7 @@
             src_ref=edge_pack,
             dst_ref=edge_packs.at[i],
             send_sem=send_sem,
-            recv_sem=edge_packs_rs.at[i // 3],
+            recv_sem=edge_packs_rs.at[i],
             device_id=target,
             device_id_type=MESH,
         )
@@ -330,12 +330,13 @@
         await_bytes(buffer.at[pl.ds(members.start, len(members))], sems.at[group])
         return members
 
-    for group in range(2):
-        for i in of_group(group, pack_r, pack_rs):
-            add_sources(i, pack_r.at[i])
+    for i in range(5):
+        pack_copies[i].wait_recv()
+        add_sources(i, pack_r.at[i])
     halo_wait(0, near_side)
     lap = add(lap, lap_side(0, near_side, field))
-    for i in of_group(2, pack_r, pack_rs):
+    for i in range(5, 7):
+        pack_copies[i].wait_recv()
         add_sources(i, pack_r.at[i])
     part = field * field * field - field + finish(
         [kernel_strength * a - gradient_energy * b for a, b in zip(fold(acc[...]), lap)]
@@ -384,18 +385,21 @@
     def _():
         set_column(edge_pack)
         add_sources(7, edge_pack, keep=False)
-        for i in of_group(0, edge_packs, edge_packs_rs):
+        for i in GROUPS[0]:
+            edge_pack_copies[i].wait_recv()
             add_sources(i, edge_packs.at[i], keep=False)
         await_bytes(edge_masked.at[0], edge_rs.at[2])
         set_pick(edge_pick, edge_list[...])
         set_stencil(edge_masked, edge_lane, edge_slot[...], edge_weight[...])
         theirs = edge_pack[4]
         their_lap = add(edge_lap(0, theirs, 0), edge_lap(0, theirs, 2))
-        for i in of_group(1, edge_packs, edge_packs_rs):
+        for i in GROUPS[1]:
+            edge_pack_copies[i].wait_recv()
             add_sources(i, edge_packs.at[i], keep=False)
         edge_copies[6].wait_recv()
         their_lap = add(their_lap, edge_lap(0, theirs, 1))
-        for i in of_group(2, edge_packs, edge_packs_rs):
+        for i in GROUPS[2]:
+            edge_pack_copies[i].wait_recv()
             add_sources(i, edge_packs.at[i], keep=False)
         theirs_now = theirs * theirs * theirs - theirs + finish(
             [
@@ -516,11 +520,11 @@
             pltpu.VMEM((1, own), f32),
             pltpu.SemaphoreType.DMA((3,)),
             pltpu.SemaphoreType.DMA,
-            pltpu.SemaphoreType.DMA((len(GROUPS),)),
+            pltpu.SemaphoreType.DMA((n_peers,)),
             pltpu.SemaphoreType.DMA((3, 2)),
             pltpu.SemaphoreType.DMA((len(GROUPS),)),
             pltpu.SemaphoreType.DMA((5,)),
-            pltpu.SemaphoreType.DMA((len(GROUPS),)),
+            pltpu.SemaphoreType.DMA((n_peers,)),
             pltpu.SemaphoreType.REGULAR,
         ],
         compiler_params=pltpu.CompilerParams(

time: 25.3 us -> 25.1 us (level)
  no operation moved by 1% of the time
where the time goes in v8:
time: 25.1 us; the launch traced here: 25 us
  Pallas kernels  23.7 us (94%)
  between operations  0.64 us (3%)
  local copies, waits for them, and re-layouts  0.57 us (2%)
    pallas_call x1, Pallas kernels, shards(): pl.pallas_call(functools.partial(step_kernel, n_wide, kernel_decay), out_...  23.7 us
    slice x1, local copies, waits for them, and re-layouts, shards(): return (both[:own], both[own:])  0.57 us

profile of v8, /device:TPU:8, one launch (start us, length us, event | category | flops | bytes accessed | tf_op | source)
XLA Modules:
  0.0 25.0 jit_solution(12040757077474970022)
XLA Ops:
  0.6 23.7 %shard_map.77 = f32[2,1,256]{2,1,0:T(1,128)S(1)} custom-call(f32[3,256]{1,0:T(4,128)} %pos_h.1, f32[1,256]{1,0:T(1,128)} %bitcast.4, f32[1,256]{1,0:T(1,128)} %bitcast.5, f32[64,256]{1,0:T(8,128)} %weight_h.1, s32[64,256]{1,0:T(8,128)} %slot_h.1, s32[2,256]{1,0:T(2,128)} %list_h.1), custom_call_target="tpu_custom_call" | custom-call | tf_op jit(solution)/shard_map/pallas_call | solution.py:484
  24.4 0.6 %fusion = (f32[1,1,256]{2,1,0:T(1,128)}, f32[1,1,256]{2,1,0:T(1,128)}) fusion(f32[2,1,256]{2,1,0:T(1,128)S(1)} %shard_map.77), kind=kLoop, calls=%fused_computation | loop fusion | bytes 4096 | tf_op jit(solution)/shard_map/slice | solution.py:547
